TPU v7x, 32 devices: a whole 2x2x4 slice. The times are simulated.
32 devices in a mesh: row: 4 (over z), col: 8 (over y, x, core).
Axes of the slice: x: 2, y: 2, z: 4, core: 2. Of those that a mesh axis runs over, the one named last changes fastest.
Arguments:
- features: bfloat16 [12288, 128], P(('row', 'col')), may hold values from -6 to 6
- weight: bfloat16 [128, 128], replicated, may hold values from -0.5 to 0.5
- tiles: bfloat16 [4, 2048, 128, 128], P('row', 'col'), may hold values from -0.09375 to 0.09375
- tile_dest: int32 [4, 2048], P('row', 'col'), may hold values from 0 to 23, as said below
- tile_src: int32 [4, 2048], P('row', 'col'), may hold values from 0 to 11, as said below
- tile_count: int32 [4, 8], P('row', 'col'), may hold values from 32 to 256, as said below
- source_of: int32 [12288], P(('row', 'col')), may hold values from 0 to 12287, as said below
- out_grad: bfloat16 [12288, 128], P(('row', 'col')), may hold values from -6 to 6
Outputs:
- activations: bfloat16 [12288, 128], P(('row', 'col'))
- feature_grad: bfloat16 [12288, 128], P(('row', 'col'))
- weight_grad: float32 [128, 128], replicated
Inputs may be any that keep to these rules, and one draw needn't show every extreme that they name: `tile_dest`: the slots of one device name distinct tiles. `tile_src`: the slots of one device name distinct tiles. `tile_count`: some device has all of its 256 slots live. `source_of`: a permutation of the 12288 vertices; of the 384 destination positions of each device, exactly 12 hold source vertices of each device.
All inputs are finite; a program needn't handle non-finite values.
Results may differ from a plain program's by a relative error of at most 0.017.
Values may be sent and summed in bfloat16 or wider, within the bound.
No kernel may reach another device: no remote copies, remote signals or barrier semaphores. Data moves between devices by JAX's collectives and lax.ppermute only.
A program may use at most 64 MiB of HBM per device.

v0:
```python
import functools
import math

import jax
import jax.numpy as jnp
from jax import lax
from jax.experimental import pallas as pl
from jax.experimental.pallas import tpu as pltpu
from jax.sharding import PartitionSpec as P


BF16 = jnp.bfloat16
F32 = jnp.float32
I32 = jnp.int32
LANES = 128
GRANT = 16 << 20
KEPT = 24 << 20


def xor_pairs(size, bit):
    return [(i, i ^ bit) for i in range(size)]


def dot(a, b, left=1, right=0):
    return lax.dot_general(a, b, (((left,), (right,)), ((), ())), preferred_element_type=F32)


def iota(shape, dim):
    return lax.broadcasted_iota(I32, shape, dim)


def call(body, out_shape, operands, spaces, scratch=(), flops=0, moved=0, grant=GRANT):
    single = not isinstance(out_shape, (list, tuple))
    spec = pl.BlockSpec(memory_space=pltpu.VMEM)
    return pl.pallas_call(
        body,
        out_shape=out_shape,
        in_specs=[pl.BlockSpec(memory_space=space) for space in spaces],
        out_specs=spec if single else [spec] * len(out_shape),
        scratch_shapes=list(scratch),
        compiler_params=pltpu.CompilerParams(vmem_limit_bytes=grant),
        cost_estimate=pl.CostEstimate(flops=flops, bytes_accessed=moved, transcendentals=0),
    )(*operands)


def half_place(part, me, chips):
    far = part ^ me
    return (1 - (far & 1)) * chips + (far >> 1)


def build_body(
    sizes,
    dest_hbm,
    src_hbm,
    count_ref,
    source_hbm,
    feat_hbm,
    cot_hbm,
    tiles_ref,
    dense_ref,
    table_ref,
    slot_ref,
    feat_ref,
    cot_ref,
    dest_ref,
    src_ref,
    source_ref,
    row_ref,
    col_ref,
    sem,
    near,
):
    n_row, n_col, span = sizes
    edge = tiles_ref.shape[-1]
    rows, cols = dense_ref.shape
    per = cols // (n_row * edge)
    chunk = 2 * edge
    my_row = lax.axis_index("row")
    my_col = lax.axis_index("col")
    loads = [
        pltpu.make_async_copy(dest_hbm, dest_ref, near.at[0]),
        pltpu.make_async_copy(src_hbm, src_ref, near.at[1]),
        pltpu.make_async_copy(source_hbm, source_ref, near.at[2]),
    ]
    rows_in = [
        pltpu.make_async_copy(feat_hbm, feat_ref, near.at[3]),
        pltpu.make_async_copy(cot_hbm, cot_ref, near.at[4]),
    ]
    for load in loads + rows_in:
        load.start()
    for part in range(n_col):
        for block in range(per):
            row_ref[part * per + block] = (half_place(part, my_col, n_col // 2) * per + block) * edge
    for part in range(n_row):
        for block in range(per):
            col_ref[part * per + block] = ((part ^ my_row) * per + block) * edge

    def clear(step, carry):
        at = pl.multiple_of(step * chunk, chunk)
        dense_ref[pl.ds(at, chunk), :] = jnp.zeros((chunk, cols), BF16)
        return carry

    lax.fori_loop(0, rows // chunk, clear, 0)
    for load in loads:
        load.wait()
    live = count_ref[0, 0]

    def start(slot):
        row = pl.multiple_of(row_ref[dest_ref[0, slot]], edge)
        col = pl.multiple_of(col_ref[src_ref[0, slot]], edge)
        pltpu.make_async_copy(
            tiles_ref.at[slot], dense_ref.at[pl.ds(row, edge), pl.ds(col, edge)], sem
        ).start()

    def start_some(step, carry):
        for at in range(4):
            start(step * 4 + at)
        return carry

    def start_one(slot, carry):
        start(slot)
        return carry

    some = live >> 2
    lax.fori_loop(0, some, start_some, 0)
    lax.fori_loop(some * 4, live, start_one, 0)

    slot_work(n_row, n_col, span, source_ref, table_ref, slot_ref)
    for load in rows_in:
        load.wait()

    def arrived(count):
        part = dense_ref.at[pl.ds(0, edge), pl.ds(0, count * edge)]
        return pltpu.make_async_copy(part, part, sem)

    def wait_many(step, carry):
        arrived(8).wait()
        return carry

    def wait_one(step, carry):
        arrived(1).wait()
        return carry

    lax.fori_loop(0, live >> 3, wait_many, 0)
    lax.fori_loop(0, live & 7, wait_one, 0)


def slot_work(n_row, n_col, span, source_ref, table_ref, slot_ref):
    rows = source_ref.shape[-1]
    slots = table_ref.shape[-1]
    n_all = n_row * n_col
    my_row = lax.axis_index("row")
    my_col = lax.axis_index("col")
    source = source_ref[...].reshape(1, rows)
    owner = ((source.astype(F32) + 0.5) * (1.0 / rows)).astype(I32)
    place = source - owner * rows + 1
    mine = iota((n_all, rows), 0) == owner
    before = (iota((rows, rows), 0) < iota((rows, rows), 1)).astype(BF16)
    earlier = dot(mine.astype(BF16), before)
    rank = jnp.sum(jnp.where(mine, earlier, 0.0), axis=0, keepdims=True).astype(I32)
    shift = n_col.bit_length() - 1
    far_row = (owner >> shift) ^ my_row
    far_col = (owner & (n_col - 1)) ^ my_col
    by_row = (far_row * n_col + far_col) * span + rank
    by_col = (far_col * n_row + far_row) * span + rank
    hot = (iota((slots, rows), 0) == by_row).astype(BF16)
    high = jnp.broadcast_to((place >> 7).astype(F32), (8, rows)).astype(BF16)
    low = jnp.broadcast_to((place & 127).astype(F32), (8, rows)).astype(BF16)
    table_ref[...] = (dot(high, hot, 1, 1) * 128.0 + dot(low, hot, 1, 1)).astype(I32)
    slot_ref[...] = jnp.where(iota((8, rows), 0) == 0, by_row, by_col)


def pick_body(n_row, n_col, span, table_ref, *refs):
    og = refs[:n_row]
    sides = refs[n_row:]
    rows = og[0].shape[0]
    lanes = n_col * span
    for r in range(n_row):
        place = table_ref[0:1, r * lanes : (r + 1) * lanes]
        hot = (iota((rows, lanes), 0) + 1 == place).astype(BF16)
        picked = dot(hot, og[r][...], 0, 0).astype(BF16)
        for k in range(n_col):
            at = ((k >> 1) * n_row + r) * span
            sides[k & 1][at : at + span, :] = picked[k * span : (k + 1) * span, :]


def pair_body(near_ref, far_ref, *out):
    size = out[0].shape[0] // 2
    for q, ref in enumerate(out):
        ref[:size, :] = near_ref[q * size : (q + 1) * size, :]
        ref[size:, :] = far_ref[q * size : (q + 1) * size, :]


def tree_sum(terms):
    terms = [term.astype(F32) for term in terms]
    while len(terms) > 1:
        terms = [terms[at] + terms[at + 1] for at in range(0, len(terms), 2)]
    return terms[0]


def forward_body(first, dense_ref, *refs):
    out = refs[-1]
    feat = jnp.concatenate([ref[...] for ref in refs[:-1]], axis=0)
    count = out.shape[0]
    step = 512 if count % 512 == 0 else 128
    for at in range(0, count, step):
        out[at : at + step, :] = dot(dense_ref[first + at : first + at + step, :], feat).astype(BF16)


def combine_body(own_ref, got_ref, *out):
    rows = out[0].shape[0]
    for at, ref in enumerate(out):
        part = slice(at * rows, (at + 1) * rows)
        ref[...] = (own_ref[part, :].astype(F32) + got_ref[part, :].astype(F32)).astype(BF16)


def middle_body(n_row, chips, slot_ref, table_ref, weight_ref, *refs):
    got = refs[:chips]
    back = refs[chips : 2 * chips]
    grad_ref = refs[2 * chips]
    out = refs[2 * chips + 1 :]
    rows, width = grad_ref.shape
    slots = table_ref.shape[1]
    lanes = slots // n_row
    marks = out[0].shape[0] - lanes - width
    mixed = got[0][...].astype(F32)
    for ref in got[1:]:
        mixed = mixed + ref[...].astype(F32)
    mixed = mixed.astype(BF16)
    pre = dot(mixed, weight_ref[...]).astype(BF16).astype(F32)
    sigma = jax.nn.sigmoid(pre)
    act = (pre * sigma).astype(BF16)
    returned = jnp.concatenate([ref[...] for ref in back], axis=0)
    hot = (iota((slots, rows), 0) == slot_ref[1:2, :]).astype(BF16)
    dest_grad = dot(hot, returned, 0, 0)
    grad = (dest_grad * (sigma * (1.0 + pre * (1.0 - sigma)))).astype(BF16)
    grad_ref[...] = grad
    hot = (iota((slots, rows), 0) == slot_ref[0:1, :]).astype(BF16)
    sent = dot(hot, act).astype(BF16)
    term = dot(mixed, grad, 0, 0).astype(BF16)
    row = iota((marks, LANES), 0)
    for r in range(n_row):
        out[r][:lanes, :] = sent[r * lanes : (r + 1) * lanes, :]
        block = jnp.zeros((marks, LANES), F32)
        for piece in range(lanes // LANES):
            at = r * lanes + piece * LANES
            place = table_ref[0:1, at : at + LANES]
            block = jnp.where(row == 2 * piece, (place >> 7).astype(F32), block)
            block = jnp.where(row == 2 * piece + 1, (place & 127).astype(F32), block)
        out[r][lanes : lanes + marks, :] = block.astype(BF16)
        out[r][lanes + marks :, :] = term


def side_body(n_row, n_col, span, *refs):
    got = refs[:n_row]
    sides = refs[n_row:]
    lanes = n_col * span
    width = got[0].shape[1]
    marks = got[0].shape[0] - lanes - width
    base = lanes * n_row // 2
    for r in range(n_row):
        for k in range(n_col):
            at = ((k >> 1) * n_row + r) * span
            sides[k & 1][at : at + span, :] = got[r][k * span : (k + 1) * span, :]
        for ref in sides:
            at = base + r * marks
            ref[at : at + marks, :] = got[r][lanes : lanes + marks, :]
    term = tree_sum([ref[lanes + marks :, :] for ref in got]).astype(BF16)
    for ref in sides:
        ref[base + n_row * marks :, :] = term


def chip_body(marks, near_ref, far_ref, *out):
    width = near_ref.shape[1]
    base = near_ref.shape[0] - marks - width
    size = base // len(out)
    term = (near_ref[base + marks :, :].astype(F32) + far_ref[base + marks :, :].astype(F32)).astype(BF16)
    for q, ref in enumerate(out):
        for side, src in enumerate((near_ref, far_ref)):
            ref[side * size : (side + 1) * size, :] = src[q * size : (q + 1) * size, :]
            at = 2 * size + side * marks
            ref[at : at + marks, :] = src[base : base + marks, :]
        ref[2 * size + 2 * marks :, :] = term


def product(dense_ref, first, grads, at, size):
    grad = jnp.concatenate([ref[...].T for ref in grads], axis=1)
    return dot(grad, dense_ref[first : first + grad.shape[1], at : at + size])


def backward_near_body(first, dense_ref, *refs):
    out = refs[-1]
    width = 2 * LANES
    for at in range(0, out.shape[1], width):
        size = min(width, out.shape[1] - at)
        out[:, at : at + size] = product(dense_ref, first, refs[:-1], at, size)


def backward_far_body(chips, dense_ref, near_ref, *refs):
    grads = refs[:chips]
    out = refs[chips:]
    rows = out[0].shape[0]
    width = 2 * LANES
    for at in range(0, near_ref.shape[1], width):
        size = min(width, near_ref.shape[1] - at)
        part = product(dense_ref, 0, grads, at, size) + near_ref[:, at : at + size]
        part = part.T.astype(BF16)
        for half in range(0, size, LANES):
            r, row = divmod(at + half, rows)
            out[r][row : row + LANES, :] = part[half : half + LANES, :]


def final_body(n_row, span, marks, scale, weight_ref, *refs):
    act_ref, total_ref, grad_ref = refs[-3:]
    parts = refs[:n_row]
    got = refs[n_row:-3]
    chips = len(got)
    rows, width = act_ref.shape
    lanes = 2 * chips * span
    size = n_row * span
    total_ref[...] = tree_sum([ref[2 * size + 2 * n_row * marks :, :] for ref in got]) * scale
    act = jnp.zeros((rows, width), F32)
    lane = iota((1, LANES), 1)
    for r in range(n_row):
        held = []
        for q in range(chips):
            for side in range(2):
                at = side * size + r * span
                held.append(got[q][at : at + span, :])
        held = jnp.concatenate(held, axis=0)
        for piece in range(lanes // LANES):
            place = jnp.zeros((1, LANES), F32)
            for k in range(2 * chips):
                at = k * span - piece * LANES
                if 0 <= at < LANES:
                    base = 2 * size + (k & 1) * n_row * marks + r * marks + 2 * piece
                    pair = got[k >> 1][base - base % 8 : base - base % 8 + 8, :].astype(F32)
                    high = pair[base % 8 : base % 8 + 1, :]
                    low = pair[base % 8 + 1 : base % 8 + 2, :]
                    inside = (lane >= at) & (lane < at + span)
                    place = jnp.where(inside, high * 128.0 + low, place)
            hot = (iota((rows, LANES), 0) + 1 == place.astype(I32)).astype(BF16)
            act = act + dot(hot, held[piece * LANES : (piece + 1) * LANES, :])
    act_ref[...] = act.astype(BF16)
    hidden = tree_sum([ref[...] for ref in parts])
    grad_ref[...] = dot(hidden.astype(BF16), weight_ref[...], 1, 1).astype(BF16)


def layer(features, weight, tiles, tile_dest, tile_src, tile_count, source_of, out_grad):
    rows, width = features.shape
    edge = tiles.shape[-1]
    n_row = lax.axis_size("row")
    n_col = lax.axis_size("col")
    n_all = n_row * n_col
    chips = n_col // 2
    span = -(-(rows // n_all) // 16) * 16
    slots = n_all * span
    lanes = n_col * span
    marks = -(-2 * (lanes // LANES) // 16) * 16
    sizes = (n_row, n_col, span)
    total = n_row * rows
    half = chips * rows
    vmem = pltpu.VMEM

    def row_swap(value, bit):
        return lax.ppermute(value, "row", xor_pairs(n_row, bit))

    def col_swap(value, bit):
        return lax.ppermute(value, "col", xor_pairs(n_col, bit))

    def row_swaps(values):
        return [values[0]] + [row_swap(values[k], k) for k in range(1, n_row)]

    def chip_swaps(values):
        return [values[0]] + [col_swap(values[k], 2 * k) for k in range(1, chips)]

    def block(count, kind=BF16, across=width):
        return jax.ShapeDtypeStruct((count, across), kind)

    dense_bytes = 4 * half * total
    kept = dense_bytes <= KEPT
    grant = GRANT if kept else dense_bytes + GRANT
    hbm = pltpu.HBM
    far_memory = lambda value: pltpu.with_memory_space_constraint(value, hbm)
    dense, own_table, slot, own_feat, own_cot = call(
        functools.partial(build_body, sizes),
        [
            pltpu.VMEM((2 * half, total), BF16) if kept else block(2 * half, BF16, total),
            block(8, I32, slots),
            block(8, I32, rows),
            block(rows),
            block(rows),
        ],
        (
            far_memory(tile_dest),
            far_memory(tile_src),
            tile_count,
            far_memory(source_of),
            far_memory(features),
            far_memory(out_grad),
            far_memory(tiles.reshape(tiles.shape[1:])),
        ),
        (hbm, hbm, pltpu.SMEM, hbm, hbm, hbm, hbm),
        scratch=[
            pltpu.SMEM(tile_dest.shape, I32),
            pltpu.SMEM(tile_src.shape, I32),
            pltpu.VMEM(source_of.shape, I32),
            pltpu.SMEM((2 * half // edge,), I32),
            pltpu.SMEM((total // edge,), I32),
            pltpu.SemaphoreType.DMA,
            pltpu.SemaphoreType.DMA((5,)),
        ],
        grant=grant,
        moved=tiles.size * 2,
    )
    table = own_table
    far_col = jnp.arange(slots)[None, :] // span % n_col
    bit = 1
    while bit < n_col:
        swapped = col_swap(table, bit)
        table = jnp.where(far_col & bit != 0, swapped, table)
        bit *= 2

    group = [own_feat] + row_swaps([features] * n_row)[1:]
    cotangent = [own_cot] + row_swaps([out_grad] * n_row)[1:]

    work = 2 * half * total * width
    far = call(
        functools.partial(forward_body, 0),
        block(half),
        (dense, *group),
        (vmem,) * (1 + n_row),
        grant=grant,
        flops=work,
    )
    got_far = col_swap(far, 1)
    near = call(
        functools.partial(forward_body, half),
        block(half),
        (dense, *group),
        (vmem,) * (1 + n_row),
        grant=grant,
        flops=work,
    )
    sums = call(
        combine_body, [block(rows)] * chips, (near, got_far), (vmem,) * 2, moved=half * width * 6
    )
    sums = chip_swaps(sums)

    near_cot, far_cot = call(
        functools.partial(pick_body, *sizes),
        [block(slots // 2)] * 2,
        (table, *cotangent),
        (vmem,) * (1 + n_row),
        flops=2 * slots * rows * width,
    )
    cot = call(
        pair_body,
        [block(slots // chips)] * chips,
        (near_cot, col_swap(far_cot, 1)),
        (vmem,) * 2,
        moved=slots * width * 4,
    )
    cot = chip_swaps(cot)

    grad, *sent = call(
        functools.partial(middle_body, n_row, chips),
        [block(rows)] + [block(lanes + marks + width)] * n_row,
        (slot, own_table, weight, *sums, *cot),
        (vmem,) * (3 + 2 * chips),
        flops=4 * slots * rows * width,
    )
    strip = chip_swaps([grad] * chips)
    other = [col_swap(value, 1) for value in strip]

    sent = row_swaps(sent)
    near_act, far_act = call(
        functools.partial(side_body, *sizes),
        [block(slots // 2 + n_row * marks + width)] * 2,
        sent,
        (vmem,) * n_row,
        moved=slots * width * 4,
    )
    by_chip = call(
        functools.partial(chip_body, n_row * marks),
        [block(slots // chips + 2 * n_row * marks + width)] * chips,
        (near_act, col_swap(far_act, 1)),
        (vmem,) * 2,
        moved=slots * width * 4,
    )
    by_chip = chip_swaps(by_chip)

    part = call(
        functools.partial(backward_near_body, half),
        block(width, F32, total),
        (dense, *strip),
        (vmem,) * (1 + chips),
        grant=grant,
        flops=work,
    )
    part = call(
        functools.partial(backward_far_body, chips),
        [block(rows)] * n_row,
        (dense, part, *other),
        (vmem,) * (2 + chips),
        grant=grant,
        flops=work,
    )
    part = row_swaps(part)
    activations, weight_grad, feature_grad = call(
        functools.partial(final_body, n_row, span, marks, 1.0 / math.sqrt(rows * n_all)),
        [block(rows), block(width, F32), block(rows)],
        (weight, *part, *by_chip),
        (vmem,) * (1 + n_row + chips),
        flops=2 * (slots + width) * rows * width,
    )
    return (activations, feature_grad, weight_grad)


def solution(mesh):
    placed = (
        P(("row", "col"), None),
        P(),
        P("row", "col", None, None),
        P("row", "col"),
        P("row", "col"),
        P("row", "col"),
        P(("row", "col")),
        P(("row", "col"), None),
    )
    return jax.shard_map(
        layer,
        mesh=mesh,
        in_specs=placed,
        out_specs=(P(("row", "col"), None), P(("row", "col"), None), P()),
        check_vma=False,
    )
```

profile of v0, /device:TPU:0, one launch (start us, length us, event | category | flops | bytes accessed | tf_op | source)
XLA Modules:
  0.0 72.0 jit_solution(11774289580780114758)
XLA Ops:
  0.6 3.1 %collective-permute-start = (bf16[384,128]{1,0:T(8,128)(2,1)}, bf16[384,128]{1,0:T(8,128)(2,1)S(1)}, u32[]{:S(2)}, u32[]{:S(2)}) collective-permute-start(bf16[384,128]{1,0:T(8,128)(2,1)} %feat_hbm.1), channel_id=1, source_target_pairs={{0,8},{8,0},{16,24},{24,16},{1,9},{9,1},{17,25},{25,17},{2,10},{10... | collective-permute-start | bytes 294920 | tf_op jit(solution)/shard_map/ppermute | solution.py:366
  3.7 2.6 %collective-permute-start.1 = (bf16[384,128]{1,0:T(8,128)(2,1)}, bf16[384,128]{1,0:T(8,128)(2,1)S(1)}, u32[]{:S(2)}, u32[]{:S(2)}) collective-permute-start(bf16[384,128]{1,0:T(8,128)(2,1)} %feat_hbm.1), channel_id=1, source_target_pairs={{0,16},{8,24},{16,0},{24,8},{1,17},{9,25},{17,1},{25,9},{2,18},{10... | collective-permute-start | bytes 294920 | tf_op jit(solution)/shard_map/ppermute | solution.py:366
  7.9 2.0 %shard_map.103 = (bf16[3072,1536]{1,0:T(8,128)(2,1)S(1)}, s32[8,512]{1,0:T(8,128)S(1)}, s32[8,384]{1,0:T(8,128)S(1)}, bf16[384,128]{1,0:T(8,128)(2,1)S(1)}, bf16[384,128]{1,0:T(8,128)(2,1)S(1)}) custom-call(s32[1,256]{1,0:T(1,128)} %dest_hbm.1, s32[1,256]{1,0:T(1,128)} %src_hbm.1, s32[1,1]{1,0:T(1,128)S(6)} %copy.11.count_ref, s32[384]{0:T(512)} %source_hbm.1, ...), custom_call_target="tpu_custom_call" | custom-call | bytes 8388608 | tf_op jit(solution)/shard_map/pallas_call | solution.py:35
  11.2 1.8 %collective-permute-start.8 = (s32[8,512]{1,0:T(8,128)S(1)}, s32[8,512]{1,0:T(8,128)S(1)}, u32[]{:S(2)}, u32[]{:S(2)}) collective-permute-start(s32[8,512]{1,0:T(8,128)S(1)} %broadcast_select_fusion), channel_id=1, source_target_pairs={{0,2},{1,3},{2,0},{3,1},{4,6},{5,7},{6,4},{7,5},{8,10},{9,11},{10,... | collective-permute-start | bytes 49160 | tf_op jit(solution)/shard_map/ppermute | solution.py:369
  13.0 1.9 %collective-permute-done.8 = s32[8,512]{1,0:T(8,128)S(1)} collective-permute-done((s32[8,512]{1,0:T(8,128)S(1)}, s32[8,512]{1,0:T(8,128)S(1)}, u32[]{:S(2)}, u32[]{:S(2)}) %collective-permute-start.8) | collective-permute-done | bytes 16416 | tf_op jit(solution)/shard_map/ppermute | solution.py:369
  14.9 4.7 %collective-permute-start.11 = (bf16[384,128]{1,0:T(8,128)(2,1)}, bf16[384,128]{1,0:T(8,128)(2,1)S(1)}, u32[]{:S(2)}, u32[]{:S(2)}) collective-permute-start(bf16[384,128]{1,0:T(8,128)(2,1)} %cot_hbm.1), channel_id=1, source_target_pairs={{0,16},{8,24},{16,0},{24,8},{1,17},{9,25},{17,1},{25,9},{2,18},{10... | collective-permute-start | bytes 294920 | tf_op jit(solution)/shard_map/ppermute | solution.py:366
  20.4 1.5 %collective-permute-start.9 = (s32[8,512]{1,0:T(8,128)S(1)}, s32[8,512]{1,0:T(8,128)S(1)}, u32[]{:S(2)}, u32[]{:S(2)}) collective-permute-start(s32[8,512]{1,0:T(8,128)S(1)} %broadcast_select_fusion.1), channel_id=1, source_target_pairs={{0,4},{1,5},{2,6},{3,7},{4,0},{5,1},{6,2},{7,3},{8,12},{9,13},{10,... | collective-permute-start | bytes 49160 | tf_op jit(solution)/shard_map/ppermute | solution.py:369
  21.9 1.4 %shard_map.105 = bf16[1536,128]{1,0:T(8,128)(2,1)S(1)} custom-call(bf16[3072,1536]{1,0:T(8,128)(2,1)S(1)} %get-tuple-element.36.dense_ref, bf16[384,128]{1,0:T(8,128)(2,1)S(1)} %get-tuple-element.39.refs_0_, bf16[384,128]{1,0:T(8,128)(2,1)S(1)} %collective-permute-done.refs_1_, bf16[384,128]{1,0:T(8,128)(2,1)S(1)} %collective-permute-done.1.refs_2_, ...), custom_call_target="tpu_custom_call" | custom-call | flops 603979776 | tf_op jit(solution)/shard_map/pallas_call | solution.py:35
  24.1 2.5 %collective-permute-done.11.refs_2_ = bf16[384,128]{1,0:T(8,128)(2,1)S(1)} collective-permute-done((bf16[384,128]{1,0:T(8,128)(2,1)}, bf16[384,128]{1,0:T(8,128)(2,1)S(1)}, u32[]{:S(2)}, u32[]{:S(2)}) %collective-permute-start.11) | collective-permute-done | bytes 98336 | tf_op jit(solution)/shard_map/ppermute | solution.py:366
  27.1 1.4 %shard_map.104.own_ref = bf16[1536,128]{1,0:T(8,128)(2,1)S(1)} custom-call(bf16[3072,1536]{1,0:T(8,128)(2,1)S(1)} %get-tuple-element.36.dense_ref, bf16[384,128]{1,0:T(8,128)(2,1)S(1)} %get-tuple-element.39.refs_0_, bf16[384,128]{1,0:T(8,128)(2,1)S(1)} %collective-permute-done.refs_1_, bf16[384,128]{1,0:T(8,128)(2,1)S(1)} %collective-permute-done.1.refs_2_, ...), custom_call_target="tpu_custom_call" | custom-call | flops 603979776 | tf_op jit(solution)/shard_map/pallas_call | solution.py:35
  29.6 1.5 %collective-permute-start.5 = (bf16[384,128]{1,0:T(8,128)(2,1)S(1)}, bf16[384,128]{1,0:T(8,128)(2,1)S(1)}, u32[]{:S(2)}, u32[]{:S(2)}) collective-permute-start(bf16[384,128]{1,0:T(8,128)(2,1)S(1)} %get-tuple-element.42), channel_id=1, source_target_pairs={{0,4},{1,5},{2,6},{3,7},{4,0},{5,1},{6,2},{7,3},{8,12},{9,13},{10,... | collective-permute-start | bytes 294920 | tf_op jit(solution)/shard_map/ppermute | solution.py:369
  33.2 1.5 %collective-permute-start.15 = (bf16[128,128]{1,0:T(8,128)(2,1)S(1)}, bf16[128,128]{1,0:T(8,128)(2,1)S(1)}, u32[]{:S(2)}, u32[]{:S(2)}) collective-permute-start(bf16[128,128]{1,0:T(8,128)(2,1)S(1)} %get-tuple-element.49), channel_id=1, source_target_pairs={{0,4},{1,5},{2,6},{3,7},{4,0},{5,1},{6,2},{7,3},{8,12},{9,13},{10,... | collective-permute-start | bytes 98312 | tf_op jit(solution)/shard_map/ppermute | solution.py:369
  34.6 2.0 %collective-permute-done.14.refs_5_ = bf16[128,128]{1,0:T(8,128)(2,1)S(1)} collective-permute-done((bf16[128,128]{1,0:T(8,128)(2,1)S(1)}, bf16[128,128]{1,0:T(8,128)(2,1)S(1)}, u32[]{:S(2)}, u32[]{:S(2)}) %collective-permute-start.14) | collective-permute-done | bytes 32800 | tf_op jit(solution)/shard_map/ppermute | solution.py:369
  36.7 1.8 %collective-permute-start.16 = (bf16[128,128]{1,0:T(8,128)(2,1)S(1)}, bf16[128,128]{1,0:T(8,128)(2,1)S(1)}, u32[]{:S(2)}, u32[]{:S(2)}) collective-permute-start(bf16[128,128]{1,0:T(8,128)(2,1)S(1)} %get-tuple-element.50), channel_id=1, source_target_pairs={{0,6},{1,7},{2,4},{3,5},{4,2},{5,3},{6,0},{7,1},{8,14},{9,15},{10,... | collective-permute-start | bytes 98312 | tf_op jit(solution)/shard_map/ppermute | solution.py:369
  38.5 3.0 %collective-permute-done.16.refs_7_ = bf16[128,128]{1,0:T(8,128)(2,1)S(1)} collective-permute-done((bf16[128,128]{1,0:T(8,128)(2,1)S(1)}, bf16[128,128]{1,0:T(8,128)(2,1)S(1)}, u32[]{:S(2)}, u32[]{:S(2)}) %collective-permute-start.16) | collective-permute-done | bytes 32800 | tf_op jit(solution)/shard_map/ppermute | solution.py:369
  42.0 2.1 %collective-permute-start.27 = (bf16[272,128]{1,0:T(8,128)(2,1)S(1)}, bf16[272,128]{1,0:T(8,128)(2,1)S(1)}, u32[]{:S(2)}, u32[]{:S(2)}) collective-permute-start(bf16[272,128]{1,0:T(8,128)(2,1)S(1)} %get-tuple-element.57), channel_id=1, source_target_pairs={{0,8},{8,0},{16,24},{24,16},{1,9},{9,1},{17,25},{25,17},{2,10},{10... | collective-permute-start | bytes 208904 | tf_op jit(solution)/shard_map/ppermute | solution.py:366
  44.8 1.8 %collective-permute-start.29 = (bf16[272,128]{1,0:T(8,128)(2,1)S(1)}, bf16[272,128]{1,0:T(8,128)(2,1)S(1)}, u32[]{:S(2)}, u32[]{:S(2)}) collective-permute-start(bf16[272,128]{1,0:T(8,128)(2,1)S(1)} %get-tuple-element.59), channel_id=1, source_target_pairs={{0,24},{8,16},{16,8},{24,0},{1,25},{9,17},{17,9},{25,1},{2,26},{10... | collective-permute-start | bytes 208904 | tf_op jit(solution)/shard_map/ppermute | solution.py:366
  47.5 1.4 %collective-permute-start.18 = (bf16[384,128]{1,0:T(8,128)(2,1)S(1)}, bf16[384,128]{1,0:T(8,128)(2,1)S(1)}, u32[]{:S(2)}, u32[]{:S(2)}) collective-permute-start(bf16[384,128]{1,0:T(8,128)(2,1)S(1)} %get-tuple-element.51.refs_0_), channel_id=1, source_target_pairs={{0,4},{1,5},{2,6},{3,7},{4,0},{5,1},{6,2},{7,3},{8,12},{9,13},{10,... | collective-permute-start | bytes 294920 | tf_op jit(solution)/shard_map/ppermute | solution.py:369
  52.2 2.3 %collective-permute-done.19.refs_3_ = bf16[384,128]{1,0:T(8,128)(2,1)S(1)} collective-permute-done((bf16[384,128]{1,0:T(8,128)(2,1)S(1)}, bf16[384,128]{1,0:T(8,128)(2,1)S(1)}, u32[]{:S(2)}, u32[]{:S(2)}) %collective-permute-start.19) | collective-permute-done | bytes 98336 | tf_op jit(solution)/shard_map/ppermute | solution.py:369
  57.2 1.7 %collective-permute-start.33 = (bf16[384,128]{1,0:T(8,128)(2,1)S(1)}, bf16[384,128]{1,0:T(8,128)(2,1)S(1)}, u32[]{:S(2)}, u32[]{:S(2)}) collective-permute-start(bf16[384,128]{1,0:T(8,128)(2,1)S(1)} %get-tuple-element.65), channel_id=1, source_target_pairs={{0,6},{1,7},{2,4},{3,5},{4,2},{5,3},{6,0},{7,1},{8,14},{9,15},{10,... | collective-permute-start | bytes 294920 | tf_op jit(solution)/shard_map/ppermute | solution.py:369
  60.8 2.0 %collective-permute-start.25 = (bf16[384,128]{1,0:T(8,128)(2,1)S(1)}, bf16[384,128]{1,0:T(8,128)(2,1)S(1)}, u32[]{:S(2)}, u32[]{:S(2)}) collective-permute-start(bf16[384,128]{1,0:T(8,128)(2,1)S(1)} %get-tuple-element.54), channel_id=1, source_target_pairs={{0,16},{8,24},{16,0},{24,8},{1,17},{9,25},{17,1},{25,9},{2,18},{10... | collective-permute-start | bytes 294920 | tf_op jit(solution)/shard_map/ppermute | solution.py:366
  62.8 1.6 %collective-permute-start.26 = (bf16[384,128]{1,0:T(8,128)(2,1)S(1)}, bf16[384,128]{1,0:T(8,128)(2,1)S(1)}, u32[]{:S(2)}, u32[]{:S(2)}) collective-permute-start(bf16[384,128]{1,0:T(8,128)(2,1)S(1)} %get-tuple-element.55), channel_id=1, source_target_pairs={{0,24},{8,16},{16,8},{24,0},{1,25},{9,17},{17,9},{25,1},{2,26},{10... | collective-permute-start | bytes 294920 | tf_op jit(solution)/shard_map/ppermute | solution.py:366
  64.5 1.4 %collective-permute-done.24.refs_1_ = bf16[384,128]{1,0:T(8,128)(2,1)S(1)} collective-permute-done((bf16[384,128]{1,0:T(8,128)(2,1)S(1)}, bf16[384,128]{1,0:T(8,128)(2,1)S(1)}, u32[]{:S(2)}, u32[]{:S(2)}) %collective-permute-start.24) | collective-permute-done | bytes 98336 | tf_op jit(solution)/shard_map/ppermute | solution.py:366
  65.9 5.2 %collective-permute-done.25.refs_2_ = bf16[384,128]{1,0:T(8,128)(2,1)S(1)} collective-permute-done((bf16[384,128]{1,0:T(8,128)(2,1)S(1)}, bf16[384,128]{1,0:T(8,128)(2,1)S(1)}, u32[]{:S(2)}, u32[]{:S(2)}) %collective-permute-start.25) | collective-permute-done | bytes 98336 | tf_op jit(solution)/shard_map/ppermute | solution.py:366
  (64 shorter events, 18.3 us)
Async XLA Ops:
  0.6 19.0 %collective-permute-start = (bf16[384,128]{1,0:T(8,128)(2,1)}, bf16[384,128]{1,0:T(8,128)(2,1)S(1)}, u32[]{:S(2)}, u32[]{:S(2)}) collective-permute-start(bf16[384,128]{1,0:T(8,128)(2,1)} %feat_hbm.1), channel_id=1, source_target_pairs={{0,8},{8,0},{16,24},{24,16},{1,9},{9,1},{17,25},{25,17},{2,10},{10... | collective-permute-start | bytes 294920 | tf_op jit(solution)/shard_map/ppermute | solution.py:366
  3.7 16.6 %collective-permute-start.1 = (bf16[384,128]{1,0:T(8,128)(2,1)}, bf16[384,128]{1,0:T(8,128)(2,1)S(1)}, u32[]{:S(2)}, u32[]{:S(2)}) collective-permute-start(bf16[384,128]{1,0:T(8,128)(2,1)} %feat_hbm.1), channel_id=1, source_target_pairs={{0,16},{8,24},{16,0},{24,8},{1,17},{9,25},{17,1},{25,9},{2,18},{10... | collective-permute-start | bytes 294920 | tf_op jit(solution)/shard_map/ppermute | solution.py:366
  6.3 15.5 %collective-permute-start.2 = (bf16[384,128]{1,0:T(8,128)(2,1)}, bf16[384,128]{1,0:T(8,128)(2,1)S(1)}, u32[]{:S(2)}, u32[]{:S(2)}) collective-permute-start(bf16[384,128]{1,0:T(8,128)(2,1)} %feat_hbm.1), channel_id=1, source_target_pairs={{0,24},{8,16},{16,8},{24,0},{1,25},{9,17},{17,9},{25,1},{2,26},{10... | collective-permute-start | bytes 294920 | tf_op jit(solution)/shard_map/ppermute | solution.py:366
  6.3 17.8 %collective-permute-start.10 = (bf16[384,128]{1,0:T(8,128)(2,1)}, bf16[384,128]{1,0:T(8,128)(2,1)S(1)}, u32[]{:S(2)}, u32[]{:S(2)}) collective-permute-start(bf16[384,128]{1,0:T(8,128)(2,1)} %cot_hbm.1), channel_id=1, source_target_pairs={{0,8},{8,0},{16,24},{24,16},{1,9},{9,1},{17,25},{25,17},{2,10},{10... | collective-permute-start | bytes 294920 | tf_op jit(solution)/shard_map/ppermute | solution.py:366
  14.9 11.7 %collective-permute-start.11 = (bf16[384,128]{1,0:T(8,128)(2,1)}, bf16[384,128]{1,0:T(8,128)(2,1)S(1)}, u32[]{:S(2)}, u32[]{:S(2)}) collective-permute-start(bf16[384,128]{1,0:T(8,128)(2,1)} %cot_hbm.1), channel_id=1, source_target_pairs={{0,16},{8,24},{16,0},{24,8},{1,17},{9,25},{17,1},{25,9},{2,18},{10... | collective-permute-start | bytes 294920 | tf_op jit(solution)/shard_map/ppermute | solution.py:366
  19.6 7.0 %collective-permute-start.12 = (bf16[384,128]{1,0:T(8,128)(2,1)}, bf16[384,128]{1,0:T(8,128)(2,1)S(1)}, u32[]{:S(2)}, u32[]{:S(2)}) collective-permute-start(bf16[384,128]{1,0:T(8,128)(2,1)} %cot_hbm.1), channel_id=1, source_target_pairs={{0,24},{8,16},{16,8},{24,0},{1,25},{9,17},{17,9},{25,1},{2,26},{10... | collective-permute-start | bytes 294920 | tf_op jit(solution)/shard_map/ppermute | solution.py:366
  23.3 5.2 %collective-permute-start.3 = (bf16[1536,128]{1,0:T(8,128)(2,1)S(1)}, bf16[1536,128]{1,0:T(8,128)(2,1)S(1)}, u32[]{:S(2)}, u32[]{:S(2)}) collective-permute-start(bf16[1536,128]{1,0:T(8,128)(2,1)S(1)} %shard_map.105), channel_id=1, source_target_pairs={{0,1},{1,0},{2,3},{3,2},{4,5},{5,4},{6,7},{7,6},{8,9},{9,8},{10,11... | collective-permute-start | bytes 1179656 | tf_op jit(solution)/shard_map/ppermute | solution.py:369
  27.0 5.1 %collective-permute-start.13 = (bf16[256,128]{1,0:T(8,128)(2,1)S(1)}, bf16[256,128]{1,0:T(8,128)(2,1)S(1)}, u32[]{:S(2)}, u32[]{:S(2)}) collective-permute-start(bf16[256,128]{1,0:T(8,128)(2,1)S(1)} %get-tuple-element.46), channel_id=1, source_target_pairs={{0,1},{1,0},{2,3},{3,2},{4,5},{5,4},{6,7},{7,6},{8,9},{9,8},{10,11... | collective-permute-start | bytes 196616 | tf_op jit(solution)/shard_map/ppermute | solution.py:369
  28.6 12.9 %collective-permute-start.4 = (bf16[384,128]{1,0:T(8,128)(2,1)S(1)}, bf16[384,128]{1,0:T(8,128)(2,1)S(1)}, u32[]{:S(2)}, u32[]{:S(2)}) collective-permute-start(bf16[384,128]{1,0:T(8,128)(2,1)S(1)} %get-tuple-element.41), channel_id=1, source_target_pairs={{0,2},{1,3},{2,0},{3,1},{4,6},{5,7},{6,4},{7,5},{8,10},{9,11},{10,... | collective-permute-start | bytes 294920 | tf_op jit(solution)/shard_map/ppermute | solution.py:369
  29.6 11.9 %collective-permute-start.5 = (bf16[384,128]{1,0:T(8,128)(2,1)S(1)}, bf16[384,128]{1,0:T(8,128)(2,1)S(1)}, u32[]{:S(2)}, u32[]{:S(2)}) collective-permute-start(bf16[384,128]{1,0:T(8,128)(2,1)S(1)} %get-tuple-element.42), channel_id=1, source_target_pairs={{0,4},{1,5},{2,6},{3,7},{4,0},{5,1},{6,2},{7,3},{8,12},{9,13},{10,... | collective-permute-start | bytes 294920 | tf_op jit(solution)/shard_map/ppermute | solution.py:369
  31.1 10.4 %collective-permute-start.6 = (bf16[384,128]{1,0:T(8,128)(2,1)S(1)}, bf16[384,128]{1,0:T(8,128)(2,1)S(1)}, u32[]{:S(2)}, u32[]{:S(2)}) collective-permute-start(bf16[384,128]{1,0:T(8,128)(2,1)S(1)} %get-tuple-element.43), channel_id=1, source_target_pairs={{0,6},{1,7},{2,4},{3,5},{4,2},{5,3},{6,0},{7,1},{8,14},{9,15},{10,... | collective-permute-start | bytes 294920 | tf_op jit(solution)/shard_map/ppermute | solution.py:369
  33.2 5.3 %collective-permute-start.15 = (bf16[128,128]{1,0:T(8,128)(2,1)S(1)}, bf16[128,128]{1,0:T(8,128)(2,1)S(1)}, u32[]{:S(2)}, u32[]{:S(2)}) collective-permute-start(bf16[128,128]{1,0:T(8,128)(2,1)S(1)} %get-tuple-element.49), channel_id=1, source_target_pairs={{0,4},{1,5},{2,6},{3,7},{4,0},{5,1},{6,2},{7,3},{8,12},{9,13},{10,... | collective-permute-start | bytes 98312 | tf_op jit(solution)/shard_map/ppermute | solution.py:369
  42.0 6.9 %collective-permute-start.27 = (bf16[272,128]{1,0:T(8,128)(2,1)S(1)}, bf16[272,128]{1,0:T(8,128)(2,1)S(1)}, u32[]{:S(2)}, u32[]{:S(2)}) collective-permute-start(bf16[272,128]{1,0:T(8,128)(2,1)S(1)} %get-tuple-element.57), channel_id=1, source_target_pairs={{0,8},{8,0},{16,24},{24,16},{1,9},{9,1},{17,25},{25,17},{2,10},{10... | collective-permute-start | bytes 208904 | tf_op jit(solution)/shard_map/ppermute | solution.py:366
  44.2 5.9 %collective-permute-start.28 = (bf16[272,128]{1,0:T(8,128)(2,1)S(1)}, bf16[272,128]{1,0:T(8,128)(2,1)S(1)}, u32[]{:S(2)}, u32[]{:S(2)}) collective-permute-start(bf16[272,128]{1,0:T(8,128)(2,1)S(1)} %get-tuple-element.58), channel_id=1, source_target_pairs={{0,16},{8,24},{16,0},{24,8},{1,17},{9,25},{17,1},{25,9},{2,18},{10... | collective-permute-start | bytes 208904 | tf_op jit(solution)/shard_map/ppermute | solution.py:366
  44.8 6.2 %collective-permute-start.29 = (bf16[272,128]{1,0:T(8,128)(2,1)S(1)}, bf16[272,128]{1,0:T(8,128)(2,1)S(1)}, u32[]{:S(2)}, u32[]{:S(2)}) collective-permute-start(bf16[272,128]{1,0:T(8,128)(2,1)S(1)} %get-tuple-element.59), channel_id=1, source_target_pairs={{0,24},{8,16},{16,8},{24,0},{1,25},{9,17},{17,9},{25,1},{2,26},{10... | collective-permute-start | bytes 208904 | tf_op jit(solution)/shard_map/ppermute | solution.py:366
  48.9 5.5 %collective-permute-start.19 = (bf16[384,128]{1,0:T(8,128)(2,1)S(1)}, bf16[384,128]{1,0:T(8,128)(2,1)S(1)}, u32[]{:S(2)}, u32[]{:S(2)}) collective-permute-start(bf16[384,128]{1,0:T(8,128)(2,1)S(1)} %get-tuple-element.51.refs_0_), channel_id=1, source_target_pairs={{0,6},{1,7},{2,4},{3,5},{4,2},{5,3},{6,0},{7,1},{8,14},{9,15},{10,... | collective-permute-start | bytes 294920 | tf_op jit(solution)/shard_map/ppermute | solution.py:369
  51.6 5.6 %collective-permute-start.21 = (bf16[384,128]{1,0:T(8,128)(2,1)S(1)}, bf16[384,128]{1,0:T(8,128)(2,1)S(1)}, u32[]{:S(2)}, u32[]{:S(2)}) collective-permute-start(bf16[384,128]{1,0:T(8,128)(2,1)S(1)} %collective-permute-done.17.refs_1_), channel_id=1, source_target_pairs={{0,1},{1,0},{2,3},{3,2},{4,5},{5,4},{6,7},{7,6},{8,9},{9,8},{10,11... | collective-permute-start | bytes 294920 | tf_op jit(solution)/shard_map/ppermute | solution.py:369
  52.1 6.8 %collective-permute-start.22 = (bf16[384,128]{1,0:T(8,128)(2,1)S(1)}, bf16[384,128]{1,0:T(8,128)(2,1)S(1)}, u32[]{:S(2)}, u32[]{:S(2)}) collective-permute-start(bf16[384,128]{1,0:T(8,128)(2,1)S(1)} %collective-permute-done.18.refs_2_), channel_id=1, source_target_pairs={{0,1},{1,0},{2,3},{3,2},{4,5},{5,4},{6,7},{7,6},{8,9},{9,8},{10,11... | collective-permute-start | bytes 294920 | tf_op jit(solution)/shard_map/ppermute | solution.py:369
  54.5 8.4 %collective-permute-start.31 = (bf16[384,128]{1,0:T(8,128)(2,1)S(1)}, bf16[384,128]{1,0:T(8,128)(2,1)S(1)}, u32[]{:S(2)}, u32[]{:S(2)}) collective-permute-start(bf16[384,128]{1,0:T(8,128)(2,1)S(1)} %get-tuple-element.63), channel_id=1, source_target_pairs={{0,2},{1,3},{2,0},{3,1},{4,6},{5,7},{6,4},{7,5},{8,10},{9,11},{10,... | collective-permute-start | bytes 294920 | tf_op jit(solution)/shard_map/ppermute | solution.py:369
  56.2 8.2 %collective-permute-start.32 = (bf16[384,128]{1,0:T(8,128)(2,1)S(1)}, bf16[384,128]{1,0:T(8,128)(2,1)S(1)}, u32[]{:S(2)}, u32[]{:S(2)}) collective-permute-start(bf16[384,128]{1,0:T(8,128)(2,1)S(1)} %get-tuple-element.64), channel_id=1, source_target_pairs={{0,4},{1,5},{2,6},{3,7},{4,0},{5,1},{6,2},{7,3},{8,12},{9,13},{10,... | collective-permute-start | bytes 294920 | tf_op jit(solution)/shard_map/ppermute | solution.py:369
  57.2 7.2 %collective-permute-start.33 = (bf16[384,128]{1,0:T(8,128)(2,1)S(1)}, bf16[384,128]{1,0:T(8,128)(2,1)S(1)}, u32[]{:S(2)}, u32[]{:S(2)}) collective-permute-start(bf16[384,128]{1,0:T(8,128)(2,1)S(1)} %get-tuple-element.65), channel_id=1, source_target_pairs={{0,6},{1,7},{2,4},{3,5},{4,2},{5,3},{6,0},{7,1},{8,14},{9,15},{10,... | collective-permute-start | bytes 294920 | tf_op jit(solution)/shard_map/ppermute | solution.py:369
  60.0 5.9 %collective-permute-start.24 = (bf16[384,128]{1,0:T(8,128)(2,1)S(1)}, bf16[384,128]{1,0:T(8,128)(2,1)S(1)}, u32[]{:S(2)}, u32[]{:S(2)}) collective-permute-start(bf16[384,128]{1,0:T(8,128)(2,1)S(1)} %get-tuple-element.53), channel_id=1, source_target_pairs={{0,8},{8,0},{16,24},{24,16},{1,9},{9,1},{17,25},{25,17},{2,10},{10... | collective-permute-start | bytes 294920 | tf_op jit(solution)/shard_map/ppermute | solution.py:366
  60.8 10.3 %collective-permute-start.25 = (bf16[384,128]{1,0:T(8,128)(2,1)S(1)}, bf16[384,128]{1,0:T(8,128)(2,1)S(1)}, u32[]{:S(2)}, u32[]{:S(2)}) collective-permute-start(bf16[384,128]{1,0:T(8,128)(2,1)S(1)} %get-tuple-element.54), channel_id=1, source_target_pairs={{0,16},{8,24},{16,0},{24,8},{1,17},{9,25},{17,1},{25,9},{2,18},{10... | collective-permute-start | bytes 294920 | tf_op jit(solution)/shard_map/ppermute | solution.py:366
  62.8 8.3 %collective-permute-start.26 = (bf16[384,128]{1,0:T(8,128)(2,1)S(1)}, bf16[384,128]{1,0:T(8,128)(2,1)S(1)}, u32[]{:S(2)}, u32[]{:S(2)}) collective-permute-start(bf16[384,128]{1,0:T(8,128)(2,1)S(1)} %get-tuple-element.55), channel_id=1, source_target_pairs={{0,24},{8,16},{16,8},{24,0},{1,25},{9,17},{17,9},{25,1},{2,26},{10... | collective-permute-start | bytes 294920 | tf_op jit(solution)/shard_map/ppermute | solution.py:366
  (11 other events, 60.4 us)
where the time goes:
time: 72.3 us; the launch traced here: 72 us
  starting transfers between devices  40.2 us (56%)
  waiting for transfers between devices  21.7 us (30%)
  Pallas kernels  8.66 us (12%)
  between operations  1.46 us (2%)
    ppermute x12, starting transfers between devices, row_swap(): return lax.ppermute(value, 'row', xor_pairs(n_row, bit))  21 us
    ppermute x22, starting transfers between devices, col_swap(): return lax.ppermute(value, 'col', xor_pairs(n_col, bit))  19.1 us
    ppermute x22, waiting for transfers between devices, col_swap(): return lax.ppermute(value, 'col', xor_pairs(n_col, bit))  11.6 us
    ppermute x12, waiting for transfers between devices, row_swap(): return lax.ppermute(value, 'row', xor_pairs(n_row, bit))  10.1 us
    pallas_call x12, Pallas kernels, call(): pl.pallas_call(body, out_shape=out_shape, in_specs=[pl.BlockSpec(memory_s...  8.66 us
  transfers between devices with their start and end apart: 34, of which 11 were waited for; matrix products, arithmetic and copies ran while one was open for 0% of the time, Pallas kernels for 10%

commit v1 on v0

--- a/solution.py
+++ b/solution.py
@@ -59,6 +59,7 @@
     tiles_ref,
     dense_ref,
     table_ref,
+    other_ref,
     slot_ref,
     feat_ref,
     cot_ref,
@@ -125,7 +126,7 @@
     lax.fori_loop(0, some, start_some, 0)
     lax.fori_loop(some * 4, live, start_one, 0)
 
-    slot_work(n_row, n_col, span, source_ref, table_ref, slot_ref)
+    slot_work(n_row, n_col, span, source_ref, table_ref, other_ref, slot_ref)
     for load in rows_in:
         load.wait()
 
@@ -145,7 +146,7 @@
     lax.fori_loop(0, live & 7, wait_one, 0)
 
 
-def slot_work(n_row, n_col, span, source_ref, table_ref, slot_ref):
+def slot_work(n_row, n_col, span, source_ref, table_ref, other_ref, slot_ref):
     rows = source_ref.shape[-1]
     slots = table_ref.shape[-1]
     n_all = n_row * n_col
@@ -163,32 +164,28 @@
     far_col = (owner & (n_col - 1)) ^ my_col
     by_row = (far_row * n_col + far_col) * span + rank
     by_col = (far_col * n_row + far_row) * span + rank
-    hot = (iota((slots, rows), 0) == by_row).astype(BF16)
     high = jnp.broadcast_to((place >> 7).astype(F32), (8, rows)).astype(BF16)
     low = jnp.broadcast_to((place & 127).astype(F32), (8, rows)).astype(BF16)
-    table_ref[...] = (dot(high, hot, 1, 1) * 128.0 + dot(low, hot, 1, 1)).astype(I32)
-    slot_ref[...] = jnp.where(iota((8, rows), 0) == 0, by_row, by_col)
+    for ref, order in ((table_ref, by_row), (other_ref, by_col)):
+        hot = (iota((slots, rows), 0) == order).astype(BF16)
+        ref[...] = (dot(high, hot, 1, 1) * 128.0 + dot(low, hot, 1, 1)).astype(I32)
+    slot_ref[...] = jnp.broadcast_to(by_row, (8, rows))
 
 
 def pick_body(n_row, n_col, span, table_ref, *refs):
-    og = refs[:n_row]
-    sides = refs[n_row:]
-    rows = og[0].shape[0]
-    lanes = n_col * span
-    for r in range(n_row):
-        place = table_ref[0:1, r * lanes : (r + 1) * lanes]
-        hot = (iota((rows, lanes), 0) + 1 == place).astype(BF16)
-        picked = dot(hot, og[r][...], 0, 0).astype(BF16)
-        for k in range(n_col):
-            at = ((k >> 1) * n_row + r) * span
-            sides[k & 1][at : at + span, :] = picked[k * span : (k + 1) * span, :]
-
-
-def pair_body(near_ref, far_ref, *out):
-    size = out[0].shape[0] // 2
-    for q, ref in enumerate(out):
-        ref[:size, :] = near_ref[q * size : (q + 1) * size, :]
-        ref[size:, :] = far_ref[q * size : (q + 1) * size, :]
+    cot = refs[:n_col]
+    out = refs[n_col:]
+    rows = cot[0].shape[0]
+    tail = n_row * span
+    for base in range(0, n_col * tail, LANES):
+        place = table_ref[0:1, base : base + LANES]
+        hot = (iota((rows, LANES), 0) + 1 == place).astype(BF16)
+        for k in range(base // tail, -(-(base + LANES) // tail)):
+            picked = dot(hot, cot[(k >> 1) + (k & 1) * (n_col // 2)][...], 0, 0).astype(BF16)
+            for r in range(n_row):
+                at = k * tail + r * span - base
+                if 0 <= at < LANES:
+                    out[r][k * span : (k + 1) * span, :] = picked[at : at + span, :]
 
 
 def tree_sum(terms):
@@ -216,9 +213,9 @@
 
 def middle_body(n_row, chips, slot_ref, table_ref, weight_ref, *refs):
     got = refs[:chips]
-    back = refs[chips : 2 * chips]
-    grad_ref = refs[2 * chips]
-    out = refs[2 * chips + 1 :]
+    back = refs[chips : chips + n_row]
+    grad_ref = refs[chips + n_row]
+    out = refs[chips + n_row + 1 :]
     rows, width = grad_ref.shape
     slots = table_ref.shape[1]
     lanes = slots // n_row
@@ -231,11 +228,10 @@
     sigma = jax.nn.sigmoid(pre)
     act = (pre * sigma).astype(BF16)
     returned = jnp.concatenate([ref[...] for ref in back], axis=0)
-    hot = (iota((slots, rows), 0) == slot_ref[1:2, :]).astype(BF16)
+    hot = (iota((slots, rows), 0) == slot_ref[0:1, :]).astype(BF16)
     dest_grad = dot(hot, returned, 0, 0)
     grad = (dest_grad * (sigma * (1.0 + pre * (1.0 - sigma)))).astype(BF16)
     grad_ref[...] = grad
-    hot = (iota((slots, rows), 0) == slot_ref[0:1, :]).astype(BF16)
     sent = dot(hot, act).astype(BF16)
     term = dot(mixed, grad, 0, 0).astype(BF16)
     row = iota((marks, LANES), 0)
@@ -382,10 +378,11 @@
     grant = GRANT if kept else dense_bytes + GRANT
     hbm = pltpu.HBM
     far_memory = lambda value: pltpu.with_memory_space_constraint(value, hbm)
-    dense, own_table, slot, own_feat, own_cot = call(
+    dense, own_table, table, slot, own_feat, own_cot = call(
         functools.partial(build_body, sizes),
         [
             pltpu.VMEM((2 * half, total), BF16) if kept else block(2 * half, BF16, total),
+            block(8, I32, slots),
             block(8, I32, slots),
             block(8, I32, rows),
             block(rows),
@@ -413,16 +410,16 @@
         grant=grant,
         moved=tiles.size * 2,
     )
-    table = own_table
-    far_col = jnp.arange(slots)[None, :] // span % n_col
+    far_row = jnp.arange(slots)[None, :] // span % n_row
     bit = 1
-    while bit < n_col:
-        swapped = col_swap(table, bit)
-        table = jnp.where(far_col & bit != 0, swapped, table)
+    while bit < n_row:
+        swapped = row_swap(table, bit)
+        table = jnp.where(far_row & bit != 0, swapped, table)
         bit *= 2
 
     group = [own_feat] + row_swaps([features] * n_row)[1:]
-    cotangent = [own_cot] + row_swaps([out_grad] * n_row)[1:]
+    cotangent = [own_cot] + chip_swaps([out_grad] * chips)[1:]
+    cotangent += [col_swap(value, 1) for value in cotangent]
 
     work = 2 * half * total * width
     far = call(
@@ -447,27 +444,20 @@
     )
     sums = chip_swaps(sums)
 
-    near_cot, far_cot = call(
+    cot = call(
         functools.partial(pick_body, *sizes),
-        [block(slots // 2)] * 2,
+        [block(lanes)] * n_row,
         (table, *cotangent),
-        (vmem,) * (1 + n_row),
-        flops=2 * slots * rows * width,
-    )
-    cot = call(
-        pair_body,
-        [block(slots // chips)] * chips,
-        (near_cot, col_swap(far_cot, 1)),
-        (vmem,) * 2,
-        moved=slots * width * 4,
-    )
-    cot = chip_swaps(cot)
+        (vmem,) * (1 + n_col),
+        flops=4 * slots * rows * width,
+    )
+    cot = row_swaps(cot)
 
     grad, *sent = call(
         functools.partial(middle_body, n_row, chips),
         [block(rows)] + [block(lanes + marks + width)] * n_row,
         (slot, own_table, weight, *sums, *cot),
-        (vmem,) * (3 + 2 * chips),
+        (vmem,) * (3 + chips + n_row),
         flops=4 * slots * rows * width,
     )
     strip = chip_swaps([grad] * chips)

time: 72.3 us -> 68.8 us (0.952)
  waiting for transfers between devices: 21.7 us -> 19 us
  starting transfers between devices: 40.2 us -> 39.2 us
    ppermute x22, waiting for transfers between devices: 11.6 us -> 3.16 us  [col_swap(): return lax.ppermute(value, 'col', xor_pairs(n_col, bit))]
    ppermute x12 -> x14, waiting for transfers between devices: 10.1 us -> 15.8 us  [row_swap(): return lax.ppermute(value, 'row', xor_pairs(n_row, bit))]
    ppermute x22, starting transfers between devices: 19.1 us -> 16.8 us  [col_swap(): return lax.ppermute(value, 'col', xor_pairs(n_col, bit))]
    ppermute x12 -> x14, starting transfers between devices: 21 us -> 22.4 us  [row_swap(): return lax.ppermute(value, 'row', xor_pairs(n_row, bit))]
    pallas_call x12 -> x11, Pallas kernels: 8.66 us -> 8.8 us  [call(): pl.pallas_call(body, out_shape=out_shape, in_specs=[pl.BlockSpec(memory_s...]
  transfers between devices with their start and end apart: 34 -> 36, of which waited for: 11 -> 11; matrix products, arithmetic and copies ran while one was open for 0% -> 0% of each run, Pallas kernels for 10% -> 11%
where the time goes in v1:
time: 68.8 us; the launch traced here: 68.5 us
  starting transfers between devices  39.2 us (57%)
  waiting for transfers between devices  19 us (28%)
  Pallas kernels  8.8 us (13%)
  between operations  1.47 us (2%)
    ppermute x14, starting transfers between devices, row_swap(): return lax.ppermute(value, 'row', xor_pairs(n_row, bit))  22.4 us
    ppermute x22, starting transfers between devices, col_swap(): return lax.ppermute(value, 'col', xor_pairs(n_col, bit))  16.8 us
    ppermute x14, waiting for transfers between devices, row_swap(): return lax.ppermute(value, 'row', xor_pairs(n_row, bit))  15.8 us
    pallas_call x11, Pallas kernels, call(): pl.pallas_call(body, out_shape=out_shape, in_specs=[pl.BlockSpec(memory_s...  8.8 us
    ppermute x22, waiting for transfers between devices, col_swap(): return lax.ppermute(value, 'col', xor_pairs(n_col, bit))  3.16 us
  transfers between devices with their start and end apart: 36, of which 11 were waited for; matrix products, arithmetic and copies ran while one was open for 0% of the time, Pallas kernels for 11%

profile of v1, /device:TPU:0, one launch (start us, length us, event | category | flops | bytes accessed | tf_op | source)
XLA Modules:
  0.0 68.5 jit_solution(2741628859354238686)
XLA Ops:
  0.6 3.1 %collective-permute-start = (bf16[384,128]{1,0:T(8,128)(2,1)}, bf16[384,128]{1,0:T(8,128)(2,1)S(1)}, u32[]{:S(2)}, u32[]{:S(2)}) collective-permute-start(bf16[384,128]{1,0:T(8,128)(2,1)} %feat_hbm.1), channel_id=1, source_target_pairs={{0,8},{8,0},{16,24},{24,16},{1,9},{9,1},{17,25},{25,17},{2,10},{10... | collective-permute-start | bytes 294920 | tf_op jit(solution)/shard_map/ppermute | solution.py:362
  3.7 2.6 %collective-permute-start.1 = (bf16[384,128]{1,0:T(8,128)(2,1)}, bf16[384,128]{1,0:T(8,128)(2,1)S(1)}, u32[]{:S(2)}, u32[]{:S(2)}) collective-permute-start(bf16[384,128]{1,0:T(8,128)(2,1)} %feat_hbm.1), channel_id=1, source_target_pairs={{0,16},{8,24},{16,0},{24,8},{1,17},{9,25},{17,1},{25,9},{2,18},{10... | collective-permute-start | bytes 294920 | tf_op jit(solution)/shard_map/ppermute | solution.py:362
  6.3 1.7 %collective-permute-start.9 = (bf16[384,128]{1,0:T(8,128)(2,1)}, bf16[384,128]{1,0:T(8,128)(2,1)S(1)}, u32[]{:S(2)}, u32[]{:S(2)}) collective-permute-start(bf16[384,128]{1,0:T(8,128)(2,1)} %cot_hbm.1), channel_id=1, source_target_pairs={{0,2},{1,3},{2,0},{3,1},{4,6},{5,7},{6,4},{7,5},{8,10},{9,11},{10,... | collective-permute-start | bytes 294920 | tf_op jit(solution)/shard_map/ppermute | solution.py:365
  8.1 1.5 %collective-permute-start.10 = (bf16[384,128]{1,0:T(8,128)(2,1)}, bf16[384,128]{1,0:T(8,128)(2,1)S(1)}, u32[]{:S(2)}, u32[]{:S(2)}) collective-permute-start(bf16[384,128]{1,0:T(8,128)(2,1)} %cot_hbm.1), channel_id=1, source_target_pairs={{0,4},{1,5},{2,6},{3,7},{4,0},{5,1},{6,2},{7,3},{8,12},{9,13},{10,... | collective-permute-start | bytes 294920 | tf_op jit(solution)/shard_map/ppermute | solution.py:365
  10.2 2.0 %shard_map.103 = (bf16[3072,1536]{1,0:T(8,128)(2,1)S(1)}, s32[8,512]{1,0:T(8,128)S(1)}, s32[8,512]{1,0:T(8,128)S(1)}, s32[8,384]{1,0:T(8,128)S(1)}, bf16[384,128...) custom-call(s32[1,256]{1,0:T(1,128)} %dest_hbm.1, s32[1,256]{1,0:T(1,128)} %src_hbm.1, s32[1,1]{1,0:T(1,128)S(6)} %copy.11.count_ref, ...), custom_call_target="tpu_custom_call" | custom-call | bytes 8388608 | tf_op jit(solution)/shard_map/pallas_call | solution.py:35
  14.4 1.3 %collective-permute-start.7 = (s32[8,512]{1,0:T(8,128)S(1)}, s32[8,512]{1,0:T(8,128)S(1)}, u32[]{:S(2)}, u32[]{:S(2)}) collective-permute-start(s32[8,512]{1,0:T(8,128)S(1)} %get-tuple-element.43), channel_id=1, source_target_pairs={{0,8},{8,0},{16,24},{24,16},{1,9},{9,1},{17,25},{25,17},{2,10},{10... | collective-permute-start | bytes 49160 | tf_op jit(solution)/shard_map/ppermute | solution.py:362
  15.7 1.4 %shard_map.105 = bf16[1536,128]{1,0:T(8,128)(2,1)S(1)} custom-call(bf16[3072,1536]{1,0:T(8,128)(2,1)S(1)} %get-tuple-element.35.dense_ref, bf16[384,128]{1,0:T(8,128)(2,1)S(1)} %get-tuple-element.38.refs_0_, bf16[384,128]{1,0:T(8,128)(2,1)S(1)} %collective-permute-done.refs_1_, bf16[384,128]{1,0:T(8,128)(2,1)S(1)} %collective-permute-done.1.refs_2_, ...), custom_call_target="tpu_custom_call" | custom-call | flops 603979776 | tf_op jit(solution)/shard_map/pallas_call | solution.py:35
  19.7 1.4 %shard_map.104.own_ref = bf16[1536,128]{1,0:T(8,128)(2,1)S(1)} custom-call(bf16[3072,1536]{1,0:T(8,128)(2,1)S(1)} %get-tuple-element.35.dense_ref, bf16[384,128]{1,0:T(8,128)(2,1)S(1)} %get-tuple-element.38.refs_0_, bf16[384,128]{1,0:T(8,128)(2,1)S(1)} %collective-permute-done.refs_1_, bf16[384,128]{1,0:T(8,128)(2,1)S(1)} %collective-permute-done.1.refs_2_, ...), custom_call_target="tpu_custom_call" | custom-call | flops 603979776 | tf_op jit(solution)/shard_map/pallas_call | solution.py:35
  21.8 1.6 %collective-permute-done.8 = s32[8,512]{1,0:T(8,128)S(1)} collective-permute-done((s32[8,512]{1,0:T(8,128)S(1)}, s32[8,512]{1,0:T(8,128)S(1)}, u32[]{:S(2)}, u32[]{:S(2)}) %collective-permute-start.8) | collective-permute-done | bytes 16416 | tf_op jit(solution)/shard_map/ppermute | solution.py:362
  23.4 1.5 %collective-permute-start.4 = (bf16[384,128]{1,0:T(8,128)(2,1)S(1)}, bf16[384,128]{1,0:T(8,128)(2,1)S(1)}, u32[]{:S(2)}, u32[]{:S(2)}) collective-permute-start(bf16[384,128]{1,0:T(8,128)(2,1)S(1)} %get-tuple-element.40), channel_id=1, source_target_pairs={{0,2},{1,3},{2,0},{3,1},{4,6},{5,7},{6,4},{7,5},{8,10},{9,11},{10,... | collective-permute-start | bytes 294920 | tf_op jit(solution)/shard_map/ppermute | solution.py:365
  24.9 1.5 %collective-permute-start.5 = (bf16[384,128]{1,0:T(8,128)(2,1)S(1)}, bf16[384,128]{1,0:T(8,128)(2,1)S(1)}, u32[]{:S(2)}, u32[]{:S(2)}) collective-permute-start(bf16[384,128]{1,0:T(8,128)(2,1)S(1)} %get-tuple-element.41), channel_id=1, source_target_pairs={{0,4},{1,5},{2,6},{3,7},{4,0},{5,1},{6,2},{7,3},{8,12},{9,13},{10,... | collective-permute-start | bytes 294920 | tf_op jit(solution)/shard_map/ppermute | solution.py:365
  27.3 1.3 %collective-permute-start.16 = (bf16[128,128]{1,0:T(8,128)(2,1)S(1)}, bf16[128,128]{1,0:T(8,128)(2,1)S(1)}, u32[]{:S(2)}, u32[]{:S(2)}) collective-permute-start(bf16[128,128]{1,0:T(8,128)(2,1)S(1)} %get-tuple-element.46), channel_id=1, source_target_pairs={{0,8},{8,0},{16,24},{24,16},{1,9},{9,1},{17,25},{25,17},{2,10},{10... | collective-permute-start | bytes 98312 | tf_op jit(solution)/shard_map/ppermute | solution.py:362
  28.6 1.8 %collective-permute-start.17 = (bf16[128,128]{1,0:T(8,128)(2,1)S(1)}, bf16[128,128]{1,0:T(8,128)(2,1)S(1)}, u32[]{:S(2)}, u32[]{:S(2)}) collective-permute-start(bf16[128,128]{1,0:T(8,128)(2,1)S(1)} %get-tuple-element.47), channel_id=1, source_target_pairs={{0,16},{8,24},{16,0},{24,8},{1,17},{9,25},{17,1},{25,9},{2,18},{10... | collective-permute-start | bytes 98312 | tf_op jit(solution)/shard_map/ppermute | solution.py:362
  31.3 2.4 %collective-permute-start.18 = (bf16[128,128]{1,0:T(8,128)(2,1)S(1)}, bf16[128,128]{1,0:T(8,128)(2,1)S(1)}, u32[]{:S(2)}, u32[]{:S(2)}) collective-permute-start(bf16[128,128]{1,0:T(8,128)(2,1)S(1)} %get-tuple-element.48), channel_id=1, source_target_pairs={{0,24},{8,16},{16,8},{24,0},{1,25},{9,17},{17,9},{25,1},{2,26},{10... | collective-permute-start | bytes 98312 | tf_op jit(solution)/shard_map/ppermute | solution.py:362
  34.0 3.1 %collective-permute-done.18.refs_7_ = bf16[128,128]{1,0:T(8,128)(2,1)S(1)} collective-permute-done((bf16[128,128]{1,0:T(8,128)(2,1)S(1)}, bf16[128,128]{1,0:T(8,128)(2,1)S(1)}, u32[]{:S(2)}, u32[]{:S(2)}) %collective-permute-start.18) | collective-permute-done | bytes 32800 | tf_op jit(solution)/shard_map/ppermute | solution.py:362
  37.8 3.2 %collective-permute-start.30 = (bf16[272,128]{1,0:T(8,128)(2,1)S(1)}, bf16[272,128]{1,0:T(8,128)(2,1)S(1)}, u32[]{:S(2)}, u32[]{:S(2)}) collective-permute-start(bf16[272,128]{1,0:T(8,128)(2,1)S(1)} %get-tuple-element.56), channel_id=1, source_target_pairs={{0,16},{8,24},{16,0},{24,8},{1,17},{9,25},{17,1},{25,9},{2,18},{10... | collective-permute-start | bytes 208904 | tf_op jit(solution)/shard_map/ppermute | solution.py:362
  42.2 1.5 %collective-permute-start.19 = (bf16[384,128]{1,0:T(8,128)(2,1)S(1)}, bf16[384,128]{1,0:T(8,128)(2,1)S(1)}, u32[]{:S(2)}, u32[]{:S(2)}) collective-permute-start(bf16[384,128]{1,0:T(8,128)(2,1)S(1)} %get-tuple-element.49.refs_0_), channel_id=1, source_target_pairs={{0,2},{1,3},{2,0},{3,1},{4,6},{5,7},{6,4},{7,5},{8,10},{9,11},{10,... | collective-permute-start | bytes 294920 | tf_op jit(solution)/shard_map/ppermute | solution.py:365
  43.7 1.7 %collective-permute-start.20 = (bf16[384,128]{1,0:T(8,128)(2,1)S(1)}, bf16[384,128]{1,0:T(8,128)(2,1)S(1)}, u32[]{:S(2)}, u32[]{:S(2)}) collective-permute-start(bf16[384,128]{1,0:T(8,128)(2,1)S(1)} %get-tuple-element.49.refs_0_), channel_id=1, source_target_pairs={{0,4},{1,5},{2,6},{3,7},{4,0},{5,1},{6,2},{7,3},{8,12},{9,13},{10,... | collective-permute-start | bytes 294920 | tf_op jit(solution)/shard_map/ppermute | solution.py:365
  45.7 1.4 %collective-permute-done.31.refs_3_ = bf16[272,128]{1,0:T(8,128)(2,1)S(1)} collective-permute-done((bf16[272,128]{1,0:T(8,128)(2,1)S(1)}, bf16[272,128]{1,0:T(8,128)(2,1)S(1)}, u32[]{:S(2)}, u32[]{:S(2)}) %collective-permute-start.31) | collective-permute-done | bytes 69664 | tf_op jit(solution)/shard_map/ppermute | solution.py:362
  48.3 2.6 %collective-permute-done.21.refs_3_ = bf16[384,128]{1,0:T(8,128)(2,1)S(1)} collective-permute-done((bf16[384,128]{1,0:T(8,128)(2,1)S(1)}, bf16[384,128]{1,0:T(8,128)(2,1)S(1)}, u32[]{:S(2)}, u32[]{:S(2)}) %collective-permute-start.21) | collective-permute-done | bytes 98336 | tf_op jit(solution)/shard_map/ppermute | solution.py:365
  53.0 2.5 %collective-permute-start.35 = (bf16[384,128]{1,0:T(8,128)(2,1)S(1)}, bf16[384,128]{1,0:T(8,128)(2,1)S(1)}, u32[]{:S(2)}, u32[]{:S(2)}) collective-permute-start(bf16[384,128]{1,0:T(8,128)(2,1)S(1)} %get-tuple-element.63), channel_id=1, source_target_pairs={{0,6},{1,7},{2,4},{3,5},{4,2},{5,3},{6,0},{7,1},{8,14},{9,15},{10,... | collective-permute-start | bytes 294920 | tf_op jit(solution)/shard_map/ppermute | solution.py:365
  56.6 3.4 %collective-permute-start.27 = (bf16[384,128]{1,0:T(8,128)(2,1)S(1)}, bf16[384,128]{1,0:T(8,128)(2,1)S(1)}, u32[]{:S(2)}, u32[]{:S(2)}) collective-permute-start(bf16[384,128]{1,0:T(8,128)(2,1)S(1)} %get-tuple-element.52), channel_id=1, source_target_pairs={{0,16},{8,24},{16,0},{24,8},{1,17},{9,25},{17,1},{25,9},{2,18},{10... | collective-permute-start | bytes 294920 | tf_op jit(solution)/shard_map/ppermute | solution.py:362
  61.0 1.5 %collective-permute-done.26.refs_1_ = bf16[384,128]{1,0:T(8,128)(2,1)S(1)} collective-permute-done((bf16[384,128]{1,0:T(8,128)(2,1)S(1)}, bf16[384,128]{1,0:T(8,128)(2,1)S(1)}, u32[]{:S(2)}, u32[]{:S(2)}) %collective-permute-start.26) | collective-permute-done | bytes 98336 | tf_op jit(solution)/shard_map/ppermute | solution.py:362
  62.5 5.1 %collective-permute-done.27.refs_2_ = bf16[384,128]{1,0:T(8,128)(2,1)S(1)} collective-permute-done((bf16[384,128]{1,0:T(8,128)(2,1)S(1)}, bf16[384,128]{1,0:T(8,128)(2,1)S(1)}, u32[]{:S(2)}, u32[]{:S(2)}) %collective-permute-start.27) | collective-permute-done | bytes 98336 | tf_op jit(solution)/shard_map/ppermute | solution.py:362
  (65 shorter events, 16.1 us)
Async XLA Ops:
  0.6 11.6 %collective-permute-start = (bf16[384,128]{1,0:T(8,128)(2,1)}, bf16[384,128]{1,0:T(8,128)(2,1)S(1)}, u32[]{:S(2)}, u32[]{:S(2)}) collective-permute-start(bf16[384,128]{1,0:T(8,128)(2,1)} %feat_hbm.1), channel_id=1, source_target_pairs={{0,8},{8,0},{16,24},{24,16},{1,9},{9,1},{17,25},{25,17},{2,10},{10... | collective-permute-start | bytes 294920 | tf_op jit(solution)/shard_map/ppermute | solution.py:362
  3.7 10.6 %collective-permute-start.1 = (bf16[384,128]{1,0:T(8,128)(2,1)}, bf16[384,128]{1,0:T(8,128)(2,1)S(1)}, u32[]{:S(2)}, u32[]{:S(2)}) collective-permute-start(bf16[384,128]{1,0:T(8,128)(2,1)} %feat_hbm.1), channel_id=1, source_target_pairs={{0,16},{8,24},{16,0},{24,8},{1,17},{9,25},{17,1},{25,9},{2,18},{10... | collective-permute-start | bytes 294920 | tf_op jit(solution)/shard_map/ppermute | solution.py:362
  6.3 9.3 %collective-permute-start.2 = (bf16[384,128]{1,0:T(8,128)(2,1)}, bf16[384,128]{1,0:T(8,128)(2,1)S(1)}, u32[]{:S(2)}, u32[]{:S(2)}) collective-permute-start(bf16[384,128]{1,0:T(8,128)(2,1)} %feat_hbm.1), channel_id=1, source_target_pairs={{0,24},{8,16},{16,8},{24,0},{1,25},{9,17},{17,9},{25,1},{2,26},{10... | collective-permute-start | bytes 294920 | tf_op jit(solution)/shard_map/ppermute | solution.py:362
  6.3 11.8 %collective-permute-start.9 = (bf16[384,128]{1,0:T(8,128)(2,1)}, bf16[384,128]{1,0:T(8,128)(2,1)S(1)}, u32[]{:S(2)}, u32[]{:S(2)}) collective-permute-start(bf16[384,128]{1,0:T(8,128)(2,1)} %cot_hbm.1), channel_id=1, source_target_pairs={{0,2},{1,3},{2,0},{3,1},{4,6},{5,7},{6,4},{7,5},{8,10},{9,11},{10,... | collective-permute-start | bytes 294920 | tf_op jit(solution)/shard_map/ppermute | solution.py:365
  8.1 10.6 %collective-permute-start.10 = (bf16[384,128]{1,0:T(8,128)(2,1)}, bf16[384,128]{1,0:T(8,128)(2,1)S(1)}, u32[]{:S(2)}, u32[]{:S(2)}) collective-permute-start(bf16[384,128]{1,0:T(8,128)(2,1)} %cot_hbm.1), channel_id=1, source_target_pairs={{0,4},{1,5},{2,6},{3,7},{4,0},{5,1},{6,2},{7,3},{8,12},{9,13},{10,... | collective-permute-start | bytes 294920 | tf_op jit(solution)/shard_map/ppermute | solution.py:365
  12.3 8.8 %collective-permute-start.11 = (bf16[384,128]{1,0:T(8,128)(2,1)}, bf16[384,128]{1,0:T(8,128)(2,1)S(1)}, u32[]{:S(2)}, u32[]{:S(2)}) collective-permute-start(bf16[384,128]{1,0:T(8,128)(2,1)} %cot_hbm.1), channel_id=1, source_target_pairs={{0,6},{1,7},{2,4},{3,5},{4,2},{5,3},{6,0},{7,1},{8,14},{9,15},{10,... | collective-permute-start | bytes 294920 | tf_op jit(solution)/shard_map/ppermute | solution.py:365
  18.1 6.7 %collective-permute-start.12 = (bf16[384,128]{1,0:T(8,128)(2,1)S(1)}, bf16[384,128]{1,0:T(8,128)(2,1)S(1)}, u32[]{:S(2)}, u32[]{:S(2)}) collective-permute-start(bf16[384,128]{1,0:T(8,128)(2,1)S(1)} %get-tuple-element.44.refs_0_), channel_id=1, source_target_pairs={{0,1},{1,0},{2,3},{3,2},{4,5},{5,4},{6,7},{7,6},{8,9},{9,8},{10,11... | collective-permute-start | bytes 294920 | tf_op jit(solution)/shard_map/ppermute | solution.py:365
  18.1 8.2 %collective-permute-start.13 = (bf16[384,128]{1,0:T(8,128)(2,1)S(1)}, bf16[384,128]{1,0:T(8,128)(2,1)S(1)}, u32[]{:S(2)}, u32[]{:S(2)}) collective-permute-start(bf16[384,128]{1,0:T(8,128)(2,1)S(1)} %collective-permute-done.9.refs_1_), channel_id=1, source_target_pairs={{0,1},{1,0},{2,3},{3,2},{4,5},{5,4},{6,7},{7,6},{8,9},{9,8},{10,11... | collective-permute-start | bytes 294920 | tf_op jit(solution)/shard_map/ppermute | solution.py:365
  21.1 5.7 %collective-permute-start.14 = (bf16[384,128]{1,0:T(8,128)(2,1)S(1)}, bf16[384,128]{1,0:T(8,128)(2,1)S(1)}, u32[]{:S(2)}, u32[]{:S(2)}) collective-permute-start(bf16[384,128]{1,0:T(8,128)(2,1)S(1)} %collective-permute-done.10.refs_2_), channel_id=1, source_target_pairs={{0,1},{1,0},{2,3},{3,2},{4,5},{5,4},{6,7},{7,6},{8,9},{9,8},{10,11... | collective-permute-start | bytes 294920 | tf_op jit(solution)/shard_map/ppermute | solution.py:365
  21.3 5.6 %collective-permute-start.15 = (bf16[384,128]{1,0:T(8,128)(2,1)S(1)}, bf16[384,128]{1,0:T(8,128)(2,1)S(1)}, u32[]{:S(2)}, u32[]{:S(2)}) collective-permute-start(bf16[384,128]{1,0:T(8,128)(2,1)S(1)} %collective-permute-done.11.refs_3_), channel_id=1, source_target_pairs={{0,1},{1,0},{2,3},{3,2},{4,5},{5,4},{6,7},{7,6},{8,9},{9,8},{10,11... | collective-permute-start | bytes 294920 | tf_op jit(solution)/shard_map/ppermute | solution.py:365
  23.4 13.8 %collective-permute-start.4 = (bf16[384,128]{1,0:T(8,128)(2,1)S(1)}, bf16[384,128]{1,0:T(8,128)(2,1)S(1)}, u32[]{:S(2)}, u32[]{:S(2)}) collective-permute-start(bf16[384,128]{1,0:T(8,128)(2,1)S(1)} %get-tuple-element.40), channel_id=1, source_target_pairs={{0,2},{1,3},{2,0},{3,1},{4,6},{5,7},{6,4},{7,5},{8,10},{9,11},{10,... | collective-permute-start | bytes 294920 | tf_op jit(solution)/shard_map/ppermute | solution.py:365
  24.9 12.3 %collective-permute-start.5 = (bf16[384,128]{1,0:T(8,128)(2,1)S(1)}, bf16[384,128]{1,0:T(8,128)(2,1)S(1)}, u32[]{:S(2)}, u32[]{:S(2)}) collective-permute-start(bf16[384,128]{1,0:T(8,128)(2,1)S(1)} %get-tuple-element.41), channel_id=1, source_target_pairs={{0,4},{1,5},{2,6},{3,7},{4,0},{5,1},{6,2},{7,3},{8,12},{9,13},{10,... | collective-permute-start | bytes 294920 | tf_op jit(solution)/shard_map/ppermute | solution.py:365
  26.4 10.8 %collective-permute-start.6 = (bf16[384,128]{1,0:T(8,128)(2,1)S(1)}, bf16[384,128]{1,0:T(8,128)(2,1)S(1)}, u32[]{:S(2)}, u32[]{:S(2)}) collective-permute-start(bf16[384,128]{1,0:T(8,128)(2,1)S(1)} %get-tuple-element.42), channel_id=1, source_target_pairs={{0,6},{1,7},{2,4},{3,5},{4,2},{5,3},{6,0},{7,1},{8,14},{9,15},{10,... | collective-permute-start | bytes 294920 | tf_op jit(solution)/shard_map/ppermute | solution.py:365
  31.3 5.8 %collective-permute-start.18 = (bf16[128,128]{1,0:T(8,128)(2,1)S(1)}, bf16[128,128]{1,0:T(8,128)(2,1)S(1)}, u32[]{:S(2)}, u32[]{:S(2)}) collective-permute-start(bf16[128,128]{1,0:T(8,128)(2,1)S(1)} %get-tuple-element.48), channel_id=1, source_target_pairs={{0,24},{8,16},{16,8},{24,0},{1,25},{9,17},{17,9},{25,1},{2,26},{10... | collective-permute-start | bytes 98312 | tf_op jit(solution)/shard_map/ppermute | solution.py:362
  37.8 7.7 %collective-permute-start.29 = (bf16[272,128]{1,0:T(8,128)(2,1)S(1)}, bf16[272,128]{1,0:T(8,128)(2,1)S(1)}, u32[]{:S(2)}, u32[]{:S(2)}) collective-permute-start(bf16[272,128]{1,0:T(8,128)(2,1)S(1)} %get-tuple-element.55), channel_id=1, source_target_pairs={{0,8},{8,0},{16,24},{24,16},{1,9},{9,1},{17,25},{25,17},{2,10},{10... | collective-permute-start | bytes 208904 | tf_op jit(solution)/shard_map/ppermute | solution.py:362
  37.8 7.9 %collective-permute-start.30 = (bf16[272,128]{1,0:T(8,128)(2,1)S(1)}, bf16[272,128]{1,0:T(8,128)(2,1)S(1)}, u32[]{:S(2)}, u32[]{:S(2)}) collective-permute-start(bf16[272,128]{1,0:T(8,128)(2,1)S(1)} %get-tuple-element.56), channel_id=1, source_target_pairs={{0,16},{8,24},{16,0},{24,8},{1,17},{9,25},{17,1},{25,9},{2,18},{10... | collective-permute-start | bytes 208904 | tf_op jit(solution)/shard_map/ppermute | solution.py:362
  41.0 6.1 %collective-permute-start.31 = (bf16[272,128]{1,0:T(8,128)(2,1)S(1)}, bf16[272,128]{1,0:T(8,128)(2,1)S(1)}, u32[]{:S(2)}, u32[]{:S(2)}) collective-permute-start(bf16[272,128]{1,0:T(8,128)(2,1)S(1)} %get-tuple-element.57), channel_id=1, source_target_pairs={{0,24},{8,16},{16,8},{24,0},{1,25},{9,17},{17,9},{25,1},{2,26},{10... | collective-permute-start | bytes 208904 | tf_op jit(solution)/shard_map/ppermute | solution.py:362
  48.3 7.1 %collective-permute-start.24 = (bf16[384,128]{1,0:T(8,128)(2,1)S(1)}, bf16[384,128]{1,0:T(8,128)(2,1)S(1)}, u32[]{:S(2)}, u32[]{:S(2)}) collective-permute-start(bf16[384,128]{1,0:T(8,128)(2,1)S(1)} %collective-permute-done.20.refs_2_), channel_id=1, source_target_pairs={{0,1},{1,0},{2,3},{3,2},{4,5},{5,4},{6,7},{7,6},{8,9},{9,8},{10,11... | collective-permute-start | bytes 294920 | tf_op jit(solution)/shard_map/ppermute | solution.py:365
  51.0 9.0 %collective-permute-start.33 = (bf16[384,128]{1,0:T(8,128)(2,1)S(1)}, bf16[384,128]{1,0:T(8,128)(2,1)S(1)}, u32[]{:S(2)}, u32[]{:S(2)}) collective-permute-start(bf16[384,128]{1,0:T(8,128)(2,1)S(1)} %get-tuple-element.61), channel_id=1, source_target_pairs={{0,2},{1,3},{2,0},{3,1},{4,6},{5,7},{6,4},{7,5},{8,10},{9,11},{10,... | collective-permute-start | bytes 294920 | tf_op jit(solution)/shard_map/ppermute | solution.py:365
  52.3 8.7 %collective-permute-start.34 = (bf16[384,128]{1,0:T(8,128)(2,1)S(1)}, bf16[384,128]{1,0:T(8,128)(2,1)S(1)}, u32[]{:S(2)}, u32[]{:S(2)}) collective-permute-start(bf16[384,128]{1,0:T(8,128)(2,1)S(1)} %get-tuple-element.62), channel_id=1, source_target_pairs={{0,4},{1,5},{2,6},{3,7},{4,0},{5,1},{6,2},{7,3},{8,12},{9,13},{10,... | collective-permute-start | bytes 294920 | tf_op jit(solution)/shard_map/ppermute | solution.py:365
  53.0 8.0 %collective-permute-start.35 = (bf16[384,128]{1,0:T(8,128)(2,1)S(1)}, bf16[384,128]{1,0:T(8,128)(2,1)S(1)}, u32[]{:S(2)}, u32[]{:S(2)}) collective-permute-start(bf16[384,128]{1,0:T(8,128)(2,1)S(1)} %get-tuple-element.63), channel_id=1, source_target_pairs={{0,6},{1,7},{2,4},{3,5},{4,2},{5,3},{6,0},{7,1},{8,14},{9,15},{10,... | collective-permute-start | bytes 294920 | tf_op jit(solution)/shard_map/ppermute | solution.py:365
  56.5 6.0 %collective-permute-start.26 = (bf16[384,128]{1,0:T(8,128)(2,1)S(1)}, bf16[384,128]{1,0:T(8,128)(2,1)S(1)}, u32[]{:S(2)}, u32[]{:S(2)}) collective-permute-start(bf16[384,128]{1,0:T(8,128)(2,1)S(1)} %get-tuple-element.51), channel_id=1, source_target_pairs={{0,8},{8,0},{16,24},{24,16},{1,9},{9,1},{17,25},{25,17},{2,10},{10... | collective-permute-start | bytes 294920 | tf_op jit(solution)/shard_map/ppermute | solution.py:362
  56.6 11.0 %collective-permute-start.27 = (bf16[384,128]{1,0:T(8,128)(2,1)S(1)}, bf16[384,128]{1,0:T(8,128)(2,1)S(1)}, u32[]{:S(2)}, u32[]{:S(2)}) collective-permute-start(bf16[384,128]{1,0:T(8,128)(2,1)S(1)} %get-tuple-element.52), channel_id=1, source_target_pairs={{0,16},{8,24},{16,0},{24,8},{1,17},{9,25},{17,1},{25,9},{2,18},{10... | collective-permute-start | bytes 294920 | tf_op jit(solution)/shard_map/ppermute | solution.py:362
  59.9 7.6 %collective-permute-start.28 = (bf16[384,128]{1,0:T(8,128)(2,1)S(1)}, bf16[384,128]{1,0:T(8,128)(2,1)S(1)}, u32[]{:S(2)}, u32[]{:S(2)}) collective-permute-start(bf16[384,128]{1,0:T(8,128)(2,1)S(1)} %get-tuple-element.53), channel_id=1, source_target_pairs={{0,24},{8,16},{16,8},{24,0},{1,25},{9,17},{17,9},{25,1},{2,26},{10... | collective-permute-start | bytes 294920 | tf_op jit(solution)/shard_map/ppermute | solution.py:362
  (13 other events, 77.8 us)

commit v2 on v1

--- a/solution.py
+++ b/solution.py
@@ -247,23 +247,27 @@
         out[r][lanes + marks :, :] = term
 
 
-def side_body(n_row, n_col, span, *refs):
+def side_body(n_row, n_col, span, all_marks, *refs):
     got = refs[:n_row]
     sides = refs[n_row:]
     lanes = n_col * span
     width = got[0].shape[1]
     marks = got[0].shape[0] - lanes - width
     base = lanes * n_row // 2
+    lines = 2 * (lanes // LANES)
+    row = iota((all_marks, LANES), 0)
+    block = jnp.zeros((all_marks, LANES), F32)
     for r in range(n_row):
         for k in range(n_col):
             at = ((k >> 1) * n_row + r) * span
             sides[k & 1][at : at + span, :] = got[r][k * span : (k + 1) * span, :]
-        for ref in sides:
-            at = base + r * marks
-            ref[at : at + marks, :] = got[r][lanes : lanes + marks, :]
+        held = got[r][lanes : lanes + marks, :].astype(F32)
+        for line in range(lines):
+            block = jnp.where(row == r * lines + line, held[line : line + 1, :], block)
     term = tree_sum([ref[lanes + marks :, :] for ref in got]).astype(BF16)
     for ref in sides:
-        ref[base + n_row * marks :, :] = term
+        ref[base : base + all_marks, :] = block.astype(BF16)
+        ref[base + all_marks :, :] = term
 
 
 def chip_body(marks, near_ref, far_ref, *out):
@@ -306,7 +310,7 @@
             out[r][row : row + LANES, :] = part[half : half + LANES, :]
 
 
-def final_body(n_row, span, marks, scale, weight_ref, *refs):
+def final_body(n_row, span, all_marks, scale, weight_ref, *refs):
     act_ref, total_ref, grad_ref = refs[-3:]
     parts = refs[:n_row]
     got = refs[n_row:-3]
@@ -314,7 +318,7 @@
     rows, width = act_ref.shape
     lanes = 2 * chips * span
     size = n_row * span
-    total_ref[...] = tree_sum([ref[2 * size + 2 * n_row * marks :, :] for ref in got]) * scale
+    total_ref[...] = tree_sum([ref[2 * size + 2 * all_marks :, :] for ref in got]) * scale
     act = jnp.zeros((rows, width), F32)
     lane = iota((1, LANES), 1)
     for r in range(n_row):
@@ -329,7 +333,7 @@
             for k in range(2 * chips):
                 at = k * span - piece * LANES
                 if 0 <= at < LANES:
-                    base = 2 * size + (k & 1) * n_row * marks + r * marks + 2 * piece
+                    base = 2 * size + (k & 1) * all_marks + 2 * (r * (lanes // LANES) + piece)
                     pair = got[k >> 1][base - base % 8 : base - base % 8 + 8, :].astype(F32)
                     high = pair[base % 8 : base % 8 + 1, :]
                     low = pair[base % 8 + 1 : base % 8 + 2, :]
@@ -353,6 +357,7 @@
     slots = n_all * span
     lanes = n_col * span
     marks = -(-2 * (lanes // LANES) // 16) * 16
+    all_marks = -(-2 * (slots // LANES) // 16) * 16
     sizes = (n_row, n_col, span)
     total = n_row * rows
     half = chips * rows
@@ -465,15 +470,15 @@
 
     sent = row_swaps(sent)
     near_act, far_act = call(
-        functools.partial(side_body, *sizes),
-        [block(slots // 2 + n_row * marks + width)] * 2,
+        functools.partial(side_body, *sizes, all_marks),
+        [block(slots // 2 + all_marks + width)] * 2,
         sent,
         (vmem,) * n_row,
         moved=slots * width * 4,
     )
     by_chip = call(
-        functools.partial(chip_body, n_row * marks),
-        [block(slots // chips + 2 * n_row * marks + width)] * chips,
+        functools.partial(chip_body, all_marks),
+        [block(slots // chips + 2 * all_marks + width)] * chips,
         (near_act, col_swap(far_act, 1)),
         (vmem,) * 2,
         moved=slots * width * 4,
@@ -498,7 +503,7 @@
     )
     part = row_swaps(part)
     activations, weight_grad, feature_grad = call(
-        functools.partial(final_body, n_row, span, marks, 1.0 / math.sqrt(rows * n_all)),
+        functools.partial(final_body, n_row, span, all_marks, 1.0 / math.sqrt(rows * n_all)),
         [block(rows), block(width, F32), block(rows)],
         (weight, *part, *by_chip),
         (vmem,) * (1 + n_row + chips),

time: 68.8 us -> 68.2 us (level)
  waiting for transfers between devices: 19 us -> 18 us
    ppermute x14, waiting for transfers between devices: 15.8 us -> 12.8 us  [row_swap(): return lax.ppermute(value, 'row', xor_pairs(n_row, bit))]
    ppermute x22, waiting for transfers between devices: 3.16 us -> 5.19 us  [col_swap(): return lax.ppermute(value, 'col', xor_pairs(n_col, bit))]
  transfers between devices with their start and end apart: 36 -> 36, of which waited for: 11 -> 10; matrix products, arithmetic and copies ran while one was open for 0% -> 0% of each run, Pallas kernels for 11% -> 11%
where the time goes in v2:
time: 68.2 us; the launch traced here: 68 us
  starting transfers between devices  39.7 us (58%)
  waiting for transfers between devices  18 us (26%)
  Pallas kernels  8.84 us (13%)
  between operations  1.48 us (2%)
    ppermute x14, starting transfers between devices, row_swap(): return lax.ppermute(value, 'row', xor_pairs(n_row, bit))  22.4 us
    ppermute x22, starting transfers between devices, col_swap(): return lax.ppermute(value, 'col', xor_pairs(n_col, bit))  17.3 us
    ppermute x14, waiting for transfers between devices, row_swap(): return lax.ppermute(value, 'row', xor_pairs(n_row, bit))  12.8 us
    pallas_call x11, Pallas kernels, call(): pl.pallas_call(body, out_shape=out_shape, in_specs=[pl.BlockSpec(memory_s...  8.84 us
    ppermute x22, waiting for transfers between devices, col_swap(): return lax.ppermute(value, 'col', xor_pairs(n_col, bit))  5.19 us
  transfers between devices with their start and end apart: 36, of which 10 were waited for; matrix products, arithmetic and copies ran while one was open for 0% of the time, Pallas kernels for 11%

profile of v2, /device:TPU:0, one launch (start us, length us, event | category | flops | bytes accessed | tf_op | source)
XLA Modules:
  0.0 68.0 jit_solution(9966060991149502515)
XLA Ops:
  0.6 3.1 %collective-permute-start = (bf16[384,128]{1,0:T(8,128)(2,1)}, bf16[384,128]{1,0:T(8,128)(2,1)S(1)}, u32[]{:S(2)}, u32[]{:S(2)}) collective-permute-start(bf16[384,128]{1,0:T(8,128)(2,1)} %feat_hbm.1), channel_id=1, source_target_pairs={{0,8},{8,0},{16,24},{24,16},{1,9},{9,1},{17,25},{25,17},{2,10},{10... | collective-permute-start | bytes 294920 | tf_op jit(solution)/shard_map/ppermute | solution.py:367
  3.7 2.6 %collective-permute-start.1 = (bf16[384,128]{1,0:T(8,128)(2,1)}, bf16[384,128]{1,0:T(8,128)(2,1)S(1)}, u32[]{:S(2)}, u32[]{:S(2)}) collective-permute-start(bf16[384,128]{1,0:T(8,128)(2,1)} %feat_hbm.1), channel_id=1, source_target_pairs={{0,16},{8,24},{16,0},{24,8},{1,17},{9,25},{17,1},{25,9},{2,18},{10... | collective-permute-start | bytes 294920 | tf_op jit(solution)/shard_map/ppermute | solution.py:367
  6.3 1.7 %collective-permute-start.9 = (bf16[384,128]{1,0:T(8,128)(2,1)}, bf16[384,128]{1,0:T(8,128)(2,1)S(1)}, u32[]{:S(2)}, u32[]{:S(2)}) collective-permute-start(bf16[384,128]{1,0:T(8,128)(2,1)} %cot_hbm.1), channel_id=1, source_target_pairs={{0,2},{1,3},{2,0},{3,1},{4,6},{5,7},{6,4},{7,5},{8,10},{9,11},{10,... | collective-permute-start | bytes 294920 | tf_op jit(solution)/shard_map/ppermute | solution.py:370
  8.1 1.5 %collective-permute-start.10 = (bf16[384,128]{1,0:T(8,128)(2,1)}, bf16[384,128]{1,0:T(8,128)(2,1)S(1)}, u32[]{:S(2)}, u32[]{:S(2)}) collective-permute-start(bf16[384,128]{1,0:T(8,128)(2,1)} %cot_hbm.1), channel_id=1, source_target_pairs={{0,4},{1,5},{2,6},{3,7},{4,0},{5,1},{6,2},{7,3},{8,12},{9,13},{10,... | collective-permute-start | bytes 294920 | tf_op jit(solution)/shard_map/ppermute | solution.py:370
  10.2 2.0 %shard_map.103 = (bf16[3072,1536]{1,0:T(8,128)(2,1)S(1)}, s32[8,512]{1,0:T(8,128)S(1)}, s32[8,512]{1,0:T(8,128)S(1)}, s32[8,384]{1,0:T(8,128)S(1)}, bf16[384,128...) custom-call(s32[1,256]{1,0:T(1,128)} %dest_hbm.1, s32[1,256]{1,0:T(1,128)} %src_hbm.1, s32[1,1]{1,0:T(1,128)S(6)} %copy.11.count_ref, ...), custom_call_target="tpu_custom_call" | custom-call | bytes 8388608 | tf_op jit(solution)/shard_map/pallas_call | solution.py:35
  15.7 1.4 %shard_map.105 = bf16[1536,128]{1,0:T(8,128)(2,1)S(1)} custom-call(bf16[3072,1536]{1,0:T(8,128)(2,1)S(1)} %get-tuple-element.35.dense_ref, bf16[384,128]{1,0:T(8,128)(2,1)S(1)} %get-tuple-element.38.refs_0_, bf16[384,128]{1,0:T(8,128)(2,1)S(1)} %collective-permute-done.refs_1_, bf16[384,128]{1,0:T(8,128)(2,1)S(1)} %collective-permute-done.1.refs_2_, ...), custom_call_target="tpu_custom_call" | custom-call | flops 603979776 | tf_op jit(solution)/shard_map/pallas_call | solution.py:35
  19.7 1.4 %shard_map.104.own_ref = bf16[1536,128]{1,0:T(8,128)(2,1)S(1)} custom-call(bf16[3072,1536]{1,0:T(8,128)(2,1)S(1)} %get-tuple-element.35.dense_ref, bf16[384,128]{1,0:T(8,128)(2,1)S(1)} %get-tuple-element.38.refs_0_, bf16[384,128]{1,0:T(8,128)(2,1)S(1)} %collective-permute-done.refs_1_, bf16[384,128]{1,0:T(8,128)(2,1)S(1)} %collective-permute-done.1.refs_2_, ...), custom_call_target="tpu_custom_call" | custom-call | flops 603979776 | tf_op jit(solution)/shard_map/pallas_call | solution.py:35
  21.8 1.6 %collective-permute-done.8 = s32[8,512]{1,0:T(8,128)S(1)} collective-permute-done((s32[8,512]{1,0:T(8,128)S(1)}, s32[8,512]{1,0:T(8,128)S(1)}, u32[]{:S(2)}, u32[]{:S(2)}) %collective-permute-start.8) | collective-permute-done | bytes 16416 | tf_op jit(solution)/shard_map/ppermute | solution.py:367
  23.4 1.5 %collective-permute-start.4 = (bf16[384,128]{1,0:T(8,128)(2,1)S(1)}, bf16[384,128]{1,0:T(8,128)(2,1)S(1)}, u32[]{:S(2)}, u32[]{:S(2)}) collective-permute-start(bf16[384,128]{1,0:T(8,128)(2,1)S(1)} %get-tuple-element.40), channel_id=1, source_target_pairs={{0,2},{1,3},{2,0},{3,1},{4,6},{5,7},{6,4},{7,5},{8,10},{9,11},{10,... | collective-permute-start | bytes 294920 | tf_op jit(solution)/shard_map/ppermute | solution.py:370
  24.9 1.5 %collective-permute-start.5 = (bf16[384,128]{1,0:T(8,128)(2,1)S(1)}, bf16[384,128]{1,0:T(8,128)(2,1)S(1)}, u32[]{:S(2)}, u32[]{:S(2)}) collective-permute-start(bf16[384,128]{1,0:T(8,128)(2,1)S(1)} %get-tuple-element.41), channel_id=1, source_target_pairs={{0,4},{1,5},{2,6},{3,7},{4,0},{5,1},{6,2},{7,3},{8,12},{9,13},{10,... | collective-permute-start | bytes 294920 | tf_op jit(solution)/shard_map/ppermute | solution.py:370
  27.3 1.3 %collective-permute-start.16 = (bf16[128,128]{1,0:T(8,128)(2,1)S(1)}, bf16[128,128]{1,0:T(8,128)(2,1)S(1)}, u32[]{:S(2)}, u32[]{:S(2)}) collective-permute-start(bf16[128,128]{1,0:T(8,128)(2,1)S(1)} %get-tuple-element.46), channel_id=1, source_target_pairs={{0,8},{8,0},{16,24},{24,16},{1,9},{9,1},{17,25},{25,17},{2,10},{10... | collective-permute-start | bytes 98312 | tf_op jit(solution)/shard_map/ppermute | solution.py:367
  28.6 1.8 %collective-permute-start.17 = (bf16[128,128]{1,0:T(8,128)(2,1)S(1)}, bf16[128,128]{1,0:T(8,128)(2,1)S(1)}, u32[]{:S(2)}, u32[]{:S(2)}) collective-permute-start(bf16[128,128]{1,0:T(8,128)(2,1)S(1)} %get-tuple-element.47), channel_id=1, source_target_pairs={{0,16},{8,24},{16,0},{24,8},{1,17},{9,25},{17,1},{25,9},{2,18},{10... | collective-permute-start | bytes 98312 | tf_op jit(solution)/shard_map/ppermute | solution.py:367
  31.3 2.4 %collective-permute-start.18 = (bf16[128,128]{1,0:T(8,128)(2,1)S(1)}, bf16[128,128]{1,0:T(8,128)(2,1)S(1)}, u32[]{:S(2)}, u32[]{:S(2)}) collective-permute-start(bf16[128,128]{1,0:T(8,128)(2,1)S(1)} %get-tuple-element.48), channel_id=1, source_target_pairs={{0,24},{8,16},{16,8},{24,0},{1,25},{9,17},{17,9},{25,1},{2,26},{10... | collective-permute-start | bytes 98312 | tf_op jit(solution)/shard_map/ppermute | solution.py:367
  34.0 3.1 %collective-permute-done.18.refs_7_ = bf16[128,128]{1,0:T(8,128)(2,1)S(1)} collective-permute-done((bf16[128,128]{1,0:T(8,128)(2,1)S(1)}, bf16[128,128]{1,0:T(8,128)(2,1)S(1)}, u32[]{:S(2)}, u32[]{:S(2)}) %collective-permute-start.18) | collective-permute-done | bytes 32800 | tf_op jit(solution)/shard_map/ppermute | solution.py:367
  37.8 1.6 %collective-permute-start.19 = (bf16[384,128]{1,0:T(8,128)(2,1)S(1)}, bf16[384,128]{1,0:T(8,128)(2,1)S(1)}, u32[]{:S(2)}, u32[]{:S(2)}) collective-permute-start(bf16[384,128]{1,0:T(8,128)(2,1)S(1)} %get-tuple-element.49.refs_0_), channel_id=1, source_target_pairs={{0,2},{1,3},{2,0},{3,1},{4,6},{5,7},{6,4},{7,5},{8,10},{9,11},{10,... | collective-permute-start | bytes 294920 | tf_op jit(solution)/shard_map/ppermute | solution.py:370
  39.4 1.7 %collective-permute-start.20 = (bf16[384,128]{1,0:T(8,128)(2,1)S(1)}, bf16[384,128]{1,0:T(8,128)(2,1)S(1)}, u32[]{:S(2)}, u32[]{:S(2)}) collective-permute-start(bf16[384,128]{1,0:T(8,128)(2,1)S(1)} %get-tuple-element.49.refs_0_), channel_id=1, source_target_pairs={{0,4},{1,5},{2,6},{3,7},{4,0},{5,1},{6,2},{7,3},{8,12},{9,13},{10,... | collective-permute-start | bytes 294920 | tf_op jit(solution)/shard_map/ppermute | solution.py:370
  41.4 3.1 %collective-permute-start.30 = (bf16[272,128]{1,0:T(8,128)(2,1)S(1)}, bf16[272,128]{1,0:T(8,128)(2,1)S(1)}, u32[]{:S(2)}, u32[]{:S(2)}) collective-permute-start(bf16[272,128]{1,0:T(8,128)(2,1)S(1)} %get-tuple-element.56), channel_id=1, source_target_pairs={{0,16},{8,24},{16,0},{24,8},{1,17},{9,25},{17,1},{25,9},{2,18},{10... | collective-permute-start | bytes 208904 | tf_op jit(solution)/shard_map/ppermute | solution.py:367
  46.8 3.8 %collective-permute-done.31.refs_3_ = bf16[272,128]{1,0:T(8,128)(2,1)S(1)} collective-permute-done((bf16[272,128]{1,0:T(8,128)(2,1)S(1)}, bf16[272,128]{1,0:T(8,128)(2,1)S(1)}, u32[]{:S(2)}, u32[]{:S(2)}) %collective-permute-start.31) | collective-permute-done | bytes 69664 | tf_op jit(solution)/shard_map/ppermute | solution.py:367
  52.7 1.7 %collective-permute-start.33 = (bf16[288,128]{1,0:T(8,128)(2,1)S(1)}, bf16[288,128]{1,0:T(8,128)(2,1)S(1)}, u32[]{:S(2)}, u32[]{:S(2)}) collective-permute-start(bf16[288,128]{1,0:T(8,128)(2,1)S(1)} %get-tuple-element.61), channel_id=1, source_target_pairs={{0,2},{1,3},{2,0},{3,1},{4,6},{5,7},{6,4},{7,5},{8,10},{9,11},{10,... | collective-permute-start | bytes 221192 | tf_op jit(solution)/shard_map/ppermute | solution.py:370
  55.6 1.7 %collective-permute-start.27 = (bf16[384,128]{1,0:T(8,128)(2,1)S(1)}, bf16[384,128]{1,0:T(8,128)(2,1)S(1)}, u32[]{:S(2)}, u32[]{:S(2)}) collective-permute-start(bf16[384,128]{1,0:T(8,128)(2,1)S(1)} %get-tuple-element.52), channel_id=1, source_target_pairs={{0,16},{8,24},{16,0},{24,8},{1,17},{9,25},{17,1},{25,9},{2,18},{10... | collective-permute-start | bytes 294920 | tf_op jit(solution)/shard_map/ppermute | solution.py:367
  57.3 2.7 %collective-permute-start.28 = (bf16[384,128]{1,0:T(8,128)(2,1)S(1)}, bf16[384,128]{1,0:T(8,128)(2,1)S(1)}, u32[]{:S(2)}, u32[]{:S(2)}) collective-permute-start(bf16[384,128]{1,0:T(8,128)(2,1)S(1)} %get-tuple-element.53), channel_id=1, source_target_pairs={{0,24},{8,16},{16,8},{24,0},{1,25},{9,17},{17,9},{25,1},{2,26},{10... | collective-permute-start | bytes 294920 | tf_op jit(solution)/shard_map/ppermute | solution.py:367
  60.0 1.8 %collective-permute-start.34 = (bf16[288,128]{1,0:T(8,128)(2,1)S(1)}, bf16[288,128]{1,0:T(8,128)(2,1)S(1)}, u32[]{:S(2)}, u32[]{:S(2)}) collective-permute-start(bf16[288,128]{1,0:T(8,128)(2,1)S(1)} %get-tuple-element.62), channel_id=1, source_target_pairs={{0,4},{1,5},{2,6},{3,7},{4,0},{5,1},{6,2},{7,3},{8,12},{9,13},{10,... | collective-permute-start | bytes 221192 | tf_op jit(solution)/shard_map/ppermute | solution.py:370
  61.9 2.5 %collective-permute-done.34.refs_6_ = bf16[288,128]{1,0:T(8,128)(2,1)S(1)} collective-permute-done((bf16[288,128]{1,0:T(8,128)(2,1)S(1)}, bf16[288,128]{1,0:T(8,128)(2,1)S(1)}, u32[]{:S(2)}, u32[]{:S(2)}) %collective-permute-start.34) | collective-permute-done | bytes 73760 | tf_op jit(solution)/shard_map/ppermute | solution.py:370
  64.3 2.7 %collective-permute-done.35.refs_7_ = bf16[288,128]{1,0:T(8,128)(2,1)S(1)} collective-permute-done((bf16[288,128]{1,0:T(8,128)(2,1)S(1)}, bf16[288,128]{1,0:T(8,128)(2,1)S(1)}, u32[]{:S(2)}, u32[]{:S(2)}) %collective-permute-start.35) | collective-permute-done | bytes 73760 | tf_op jit(solution)/shard_map/ppermute | solution.py:370
  (65 shorter events, 16.4 us)
Async XLA Ops:
  0.6 11.6 %collective-permute-start = (bf16[384,128]{1,0:T(8,128)(2,1)}, bf16[384,128]{1,0:T(8,128)(2,1)S(1)}, u32[]{:S(2)}, u32[]{:S(2)}) collective-permute-start(bf16[384,128]{1,0:T(8,128)(2,1)} %feat_hbm.1), channel_id=1, source_target_pairs={{0,8},{8,0},{16,24},{24,16},{1,9},{9,1},{17,25},{25,17},{2,10},{10... | collective-permute-start | bytes 294920 | tf_op jit(solution)/shard_map/ppermute | solution.py:367
  3.7 10.6 %collective-permute-start.1 = (bf16[384,128]{1,0:T(8,128)(2,1)}, bf16[384,128]{1,0:T(8,128)(2,1)S(1)}, u32[]{:S(2)}, u32[]{:S(2)}) collective-permute-start(bf16[384,128]{1,0:T(8,128)(2,1)} %feat_hbm.1), channel_id=1, source_target_pairs={{0,16},{8,24},{16,0},{24,8},{1,17},{9,25},{17,1},{25,9},{2,18},{10... | collective-permute-start | bytes 294920 | tf_op jit(solution)/shard_map/ppermute | solution.py:367
  6.3 9.3 %collective-permute-start.2 = (bf16[384,128]{1,0:T(8,128)(2,1)}, bf16[384,128]{1,0:T(8,128)(2,1)S(1)}, u32[]{:S(2)}, u32[]{:S(2)}) collective-permute-start(bf16[384,128]{1,0:T(8,128)(2,1)} %feat_hbm.1), channel_id=1, source_target_pairs={{0,24},{8,16},{16,8},{24,0},{1,25},{9,17},{17,9},{25,1},{2,26},{10... | collective-permute-start | bytes 294920 | tf_op jit(solution)/shard_map/ppermute | solution.py:367
  6.3 11.8 %collective-permute-start.9 = (bf16[384,128]{1,0:T(8,128)(2,1)}, bf16[384,128]{1,0:T(8,128)(2,1)S(1)}, u32[]{:S(2)}, u32[]{:S(2)}) collective-permute-start(bf16[384,128]{1,0:T(8,128)(2,1)} %cot_hbm.1), channel_id=1, source_target_pairs={{0,2},{1,3},{2,0},{3,1},{4,6},{5,7},{6,4},{7,5},{8,10},{9,11},{10,... | collective-permute-start | bytes 294920 | tf_op jit(solution)/shard_map/ppermute | solution.py:370
  8.1 10.6 %collective-permute-start.10 = (bf16[384,128]{1,0:T(8,128)(2,1)}, bf16[384,128]{1,0:T(8,128)(2,1)S(1)}, u32[]{:S(2)}, u32[]{:S(2)}) collective-permute-start(bf16[384,128]{1,0:T(8,128)(2,1)} %cot_hbm.1), channel_id=1, source_target_pairs={{0,4},{1,5},{2,6},{3,7},{4,0},{5,1},{6,2},{7,3},{8,12},{9,13},{10,... | collective-permute-start | bytes 294920 | tf_op jit(solution)/shard_map/ppermute | solution.py:370
  12.3 8.8 %collective-permute-start.11 = (bf16[384,128]{1,0:T(8,128)(2,1)}, bf16[384,128]{1,0:T(8,128)(2,1)S(1)}, u32[]{:S(2)}, u32[]{:S(2)}) collective-permute-start(bf16[384,128]{1,0:T(8,128)(2,1)} %cot_hbm.1), channel_id=1, source_target_pairs={{0,6},{1,7},{2,4},{3,5},{4,2},{5,3},{6,0},{7,1},{8,14},{9,15},{10,... | collective-permute-start | bytes 294920 | tf_op jit(solution)/shard_map/ppermute | solution.py:370
  18.1 6.7 %collective-permute-start.12 = (bf16[384,128]{1,0:T(8,128)(2,1)S(1)}, bf16[384,128]{1,0:T(8,128)(2,1)S(1)}, u32[]{:S(2)}, u32[]{:S(2)}) collective-permute-start(bf16[384,128]{1,0:T(8,128)(2,1)S(1)} %get-tuple-element.44.refs_0_), channel_id=1, source_target_pairs={{0,1},{1,0},{2,3},{3,2},{4,5},{5,4},{6,7},{7,6},{8,9},{9,8},{10,11... | collective-permute-start | bytes 294920 | tf_op jit(solution)/shard_map/ppermute | solution.py:370
  18.1 8.2 %collective-permute-start.13 = (bf16[384,128]{1,0:T(8,128)(2,1)S(1)}, bf16[384,128]{1,0:T(8,128)(2,1)S(1)}, u32[]{:S(2)}, u32[]{:S(2)}) collective-permute-start(bf16[384,128]{1,0:T(8,128)(2,1)S(1)} %collective-permute-done.9.refs_1_), channel_id=1, source_target_pairs={{0,1},{1,0},{2,3},{3,2},{4,5},{5,4},{6,7},{7,6},{8,9},{9,8},{10,11... | collective-permute-start | bytes 294920 | tf_op jit(solution)/shard_map/ppermute | solution.py:370
  21.1 5.7 %collective-permute-start.14 = (bf16[384,128]{1,0:T(8,128)(2,1)S(1)}, bf16[384,128]{1,0:T(8,128)(2,1)S(1)}, u32[]{:S(2)}, u32[]{:S(2)}) collective-permute-start(bf16[384,128]{1,0:T(8,128)(2,1)S(1)} %collective-permute-done.10.refs_2_), channel_id=1, source_target_pairs={{0,1},{1,0},{2,3},{3,2},{4,5},{5,4},{6,7},{7,6},{8,9},{9,8},{10,11... | collective-permute-start | bytes 294920 | tf_op jit(solution)/shard_map/ppermute | solution.py:370
  21.3 5.6 %collective-permute-start.15 = (bf16[384,128]{1,0:T(8,128)(2,1)S(1)}, bf16[384,128]{1,0:T(8,128)(2,1)S(1)}, u32[]{:S(2)}, u32[]{:S(2)}) collective-permute-start(bf16[384,128]{1,0:T(8,128)(2,1)S(1)} %collective-permute-done.11.refs_3_), channel_id=1, source_target_pairs={{0,1},{1,0},{2,3},{3,2},{4,5},{5,4},{6,7},{7,6},{8,9},{9,8},{10,11... | collective-permute-start | bytes 294920 | tf_op jit(solution)/shard_map/ppermute | solution.py:370
  23.4 13.8 %collective-permute-start.4 = (bf16[384,128]{1,0:T(8,128)(2,1)S(1)}, bf16[384,128]{1,0:T(8,128)(2,1)S(1)}, u32[]{:S(2)}, u32[]{:S(2)}) collective-permute-start(bf16[384,128]{1,0:T(8,128)(2,1)S(1)} %get-tuple-element.40), channel_id=1, source_target_pairs={{0,2},{1,3},{2,0},{3,1},{4,6},{5,7},{6,4},{7,5},{8,10},{9,11},{10,... | collective-permute-start | bytes 294920 | tf_op jit(solution)/shard_map/ppermute | solution.py:370
  24.9 12.3 %collective-permute-start.5 = (bf16[384,128]{1,0:T(8,128)(2,1)S(1)}, bf16[384,128]{1,0:T(8,128)(2,1)S(1)}, u32[]{:S(2)}, u32[]{:S(2)}) collective-permute-start(bf16[384,128]{1,0:T(8,128)(2,1)S(1)} %get-tuple-element.41), channel_id=1, source_target_pairs={{0,4},{1,5},{2,6},{3,7},{4,0},{5,1},{6,2},{7,3},{8,12},{9,13},{10,... | collective-permute-start | bytes 294920 | tf_op jit(solution)/shard_map/ppermute | solution.py:370
  26.4 10.8 %collective-permute-start.6 = (bf16[384,128]{1,0:T(8,128)(2,1)S(1)}, bf16[384,128]{1,0:T(8,128)(2,1)S(1)}, u32[]{:S(2)}, u32[]{:S(2)}) collective-permute-start(bf16[384,128]{1,0:T(8,128)(2,1)S(1)} %get-tuple-element.42), channel_id=1, source_target_pairs={{0,6},{1,7},{2,4},{3,5},{4,2},{5,3},{6,0},{7,1},{8,14},{9,15},{10,... | collective-permute-start | bytes 294920 | tf_op jit(solution)/shard_map/ppermute | solution.py:370
  28.6 5.4 %collective-permute-start.17 = (bf16[128,128]{1,0:T(8,128)(2,1)S(1)}, bf16[128,128]{1,0:T(8,128)(2,1)S(1)}, u32[]{:S(2)}, u32[]{:S(2)}) collective-permute-start(bf16[128,128]{1,0:T(8,128)(2,1)S(1)} %get-tuple-element.47), channel_id=1, source_target_pairs={{0,16},{8,24},{16,0},{24,8},{1,17},{9,25},{17,1},{25,9},{2,18},{10... | collective-permute-start | bytes 98312 | tf_op jit(solution)/shard_map/ppermute | solution.py:367
  31.3 5.8 %collective-permute-start.18 = (bf16[128,128]{1,0:T(8,128)(2,1)S(1)}, bf16[128,128]{1,0:T(8,128)(2,1)S(1)}, u32[]{:S(2)}, u32[]{:S(2)}) collective-permute-start(bf16[128,128]{1,0:T(8,128)(2,1)S(1)} %get-tuple-element.48), channel_id=1, source_target_pairs={{0,24},{8,16},{16,8},{24,0},{1,25},{9,17},{17,9},{25,1},{2,26},{10... | collective-permute-start | bytes 98312 | tf_op jit(solution)/shard_map/ppermute | solution.py:367
  37.8 6.7 %collective-permute-start.29 = (bf16[272,128]{1,0:T(8,128)(2,1)S(1)}, bf16[272,128]{1,0:T(8,128)(2,1)S(1)}, u32[]{:S(2)}, u32[]{:S(2)}) collective-permute-start(bf16[272,128]{1,0:T(8,128)(2,1)S(1)} %get-tuple-element.55), channel_id=1, source_target_pairs={{0,8},{8,0},{16,24},{24,16},{1,9},{9,1},{17,25},{25,17},{2,10},{10... | collective-permute-start | bytes 208904 | tf_op jit(solution)/shard_map/ppermute | solution.py:367
  37.8 13.4 %collective-permute-start.19 = (bf16[384,128]{1,0:T(8,128)(2,1)S(1)}, bf16[384,128]{1,0:T(8,128)(2,1)S(1)}, u32[]{:S(2)}, u32[]{:S(2)}) collective-permute-start(bf16[384,128]{1,0:T(8,128)(2,1)S(1)} %get-tuple-element.49.refs_0_), channel_id=1, source_target_pairs={{0,2},{1,3},{2,0},{3,1},{4,6},{5,7},{6,4},{7,5},{8,10},{9,11},{10,... | collective-permute-start | bytes 294920 | tf_op jit(solution)/shard_map/ppermute | solution.py:370
  39.4 11.9 %collective-permute-start.20 = (bf16[384,128]{1,0:T(8,128)(2,1)S(1)}, bf16[384,128]{1,0:T(8,128)(2,1)S(1)}, u32[]{:S(2)}, u32[]{:S(2)}) collective-permute-start(bf16[384,128]{1,0:T(8,128)(2,1)S(1)} %get-tuple-element.49.refs_0_), channel_id=1, source_target_pairs={{0,4},{1,5},{2,6},{3,7},{4,0},{5,1},{6,2},{7,3},{8,12},{9,13},{10,... | collective-permute-start | bytes 294920 | tf_op jit(solution)/shard_map/ppermute | solution.py:370
  41.1 10.6 %collective-permute-start.21 = (bf16[384,128]{1,0:T(8,128)(2,1)S(1)}, bf16[384,128]{1,0:T(8,128)(2,1)S(1)}, u32[]{:S(2)}, u32[]{:S(2)}) collective-permute-start(bf16[384,128]{1,0:T(8,128)(2,1)S(1)} %get-tuple-element.49.refs_0_), channel_id=1, source_target_pairs={{0,6},{1,7},{2,4},{3,5},{4,2},{5,3},{6,0},{7,1},{8,14},{9,15},{10,... | collective-permute-start | bytes 294920 | tf_op jit(solution)/shard_map/ppermute | solution.py:370
  44.5 6.1 %collective-permute-start.31 = (bf16[272,128]{1,0:T(8,128)(2,1)S(1)}, bf16[272,128]{1,0:T(8,128)(2,1)S(1)}, u32[]{:S(2)}, u32[]{:S(2)}) collective-permute-start(bf16[272,128]{1,0:T(8,128)(2,1)S(1)} %get-tuple-element.57), channel_id=1, source_target_pairs={{0,24},{8,16},{16,8},{24,0},{1,25},{9,17},{17,9},{25,1},{2,26},{10... | collective-permute-start | bytes 208904 | tf_op jit(solution)/shard_map/ppermute | solution.py:367
  52.7 9.0 %collective-permute-start.33 = (bf16[288,128]{1,0:T(8,128)(2,1)S(1)}, bf16[288,128]{1,0:T(8,128)(2,1)S(1)}, u32[]{:S(2)}, u32[]{:S(2)}) collective-permute-start(bf16[288,128]{1,0:T(8,128)(2,1)S(1)} %get-tuple-element.61), channel_id=1, source_target_pairs={{0,2},{1,3},{2,0},{3,1},{4,6},{5,7},{6,4},{7,5},{8,10},{9,11},{10,... | collective-permute-start | bytes 221192 | tf_op jit(solution)/shard_map/ppermute | solution.py:370
  55.5 11.5 %collective-permute-start.26 = (bf16[384,128]{1,0:T(8,128)(2,1)S(1)}, bf16[384,128]{1,0:T(8,128)(2,1)S(1)}, u32[]{:S(2)}, u32[]{:S(2)}) collective-permute-start(bf16[384,128]{1,0:T(8,128)(2,1)S(1)} %get-tuple-element.51), channel_id=1, source_target_pairs={{0,8},{8,0},{16,24},{24,16},{1,9},{9,1},{17,25},{25,17},{2,10},{10... | collective-permute-start | bytes 294920 | tf_op jit(solution)/shard_map/ppermute | solution.py:367
  55.6 11.4 %collective-permute-start.27 = (bf16[384,128]{1,0:T(8,128)(2,1)S(1)}, bf16[384,128]{1,0:T(8,128)(2,1)S(1)}, u32[]{:S(2)}, u32[]{:S(2)}) collective-permute-start(bf16[384,128]{1,0:T(8,128)(2,1)S(1)} %get-tuple-element.52), channel_id=1, source_target_pairs={{0,16},{8,24},{16,0},{24,8},{1,17},{9,25},{17,1},{25,9},{2,18},{10... | collective-permute-start | bytes 294920 | tf_op jit(solution)/shard_map/ppermute | solution.py:367
  57.3 9.7 %collective-permute-start.28 = (bf16[384,128]{1,0:T(8,128)(2,1)S(1)}, bf16[384,128]{1,0:T(8,128)(2,1)S(1)}, u32[]{:S(2)}, u32[]{:S(2)}) collective-permute-start(bf16[384,128]{1,0:T(8,128)(2,1)S(1)} %get-tuple-element.53), channel_id=1, source_target_pairs={{0,24},{8,16},{16,8},{24,0},{1,25},{9,17},{17,9},{25,1},{2,26},{10... | collective-permute-start | bytes 294920 | tf_op jit(solution)/shard_map/ppermute | solution.py:367
  (13 other events, 67.9 us)

commit v3 on v2

--- a/solution.py
+++ b/solution.py
@@ -296,17 +296,18 @@
         out[:, at : at + size] = product(dense_ref, first, refs[:-1], at, size)
 
 
-def backward_far_body(chips, dense_ref, near_ref, *refs):
+def backward_far_body(chips, first, dense_ref, near_ref, *refs):
     grads = refs[:chips]
     out = refs[chips:]
     rows = out[0].shape[0]
     width = 2 * LANES
-    for at in range(0, near_ref.shape[1], width):
-        size = min(width, near_ref.shape[1] - at)
+    stop = first + len(out) * rows
+    for at in range(first, stop, width):
+        size = min(width, stop - at)
         part = product(dense_ref, 0, grads, at, size) + near_ref[:, at : at + size]
         part = part.T.astype(BF16)
         for half in range(0, size, LANES):
-            r, row = divmod(at + half, rows)
+            r, row = divmod(at + half - first, rows)
             out[r][row : row + LANES, :] = part[half : half + LANES, :]
 
 
@@ -493,14 +494,18 @@
         grant=grant,
         flops=work,
     )
-    part = call(
-        functools.partial(backward_far_body, chips),
-        [block(rows)] * n_row,
-        (dense, part, *other),
-        (vmem,) * (2 + chips),
-        grant=grant,
-        flops=work,
-    )
+    near_part = part
+    part = []
+    for first in (n_row // 2, 0):
+        blocks = call(
+            functools.partial(backward_far_body, chips, first * rows),
+            [block(rows)] * (n_row // 2),
+            (dense, near_part, *other),
+            (vmem,) * (2 + chips),
+            grant=grant,
+            flops=work // 2,
+        )
+        part = [*blocks, *part]
     part = row_swaps(part)
     activations, weight_grad, feature_grad = call(
         functools.partial(final_body, n_row, span, all_marks, 1.0 / math.sqrt(rows * n_all)),

time: 68.2 us -> 68.4 us (level)
    pallas_call x11 -> x12, Pallas kernels: 8.84 us -> 8.92 us  [call(): pl.pallas_call(body, out_shape=out_shape, in_specs=[pl.BlockSpec(memory_s...]
where the time goes in v3:
time: 68.4 us; the launch traced here: 68.1 us
  starting transfers between devices  39.7 us (58%)
  waiting for transfers between devices  18 us (26%)
  Pallas kernels  8.92 us (13%)
  between operations  1.49 us (2%)
    ppermute x14, starting transfers between devices, row_swap(): return lax.ppermute(value, 'row', xor_pairs(n_row, bit))  22.4 us
    ppermute x22, starting transfers between devices, col_swap(): return lax.ppermute(value, 'col', xor_pairs(n_col, bit))  17.3 us
    ppermute x14, waiting for transfers between devices, row_swap(): return lax.ppermute(value, 'row', xor_pairs(n_row, bit))  12.8 us
    pallas_call x12, Pallas kernels, call(): pl.pallas_call(body, out_shape=out_shape, in_specs=[pl.BlockSpec(memory_s...  8.92 us
    ppermute x22, waiting for transfers between devices, col_swap(): return lax.ppermute(value, 'col', xor_pairs(n_col, bit))  5.19 us
  transfers between devices with their start and end apart: 36, of which 10 were waited for; matrix products, arithmetic and copies ran while one was open for 0% of the time, Pallas kernels for 11%

profile of v3, /device:TPU:0, one launch (start us, length us, event | category | flops | bytes accessed | tf_op | source)
XLA Modules:
  0.0 68.1 jit_solution(15033028376685658831)
XLA Ops:
  0.6 3.1 %collective-permute-start = (bf16[384,128]{1,0:T(8,128)(2,1)}, bf16[384,128]{1,0:T(8,128)(2,1)S(1)}, u32[]{:S(2)}, u32[]{:S(2)}) collective-permute-start(bf16[384,128]{1,0:T(8,128)(2,1)} %feat_hbm.1), channel_id=1, source_target_pairs={{0,8},{8,0},{16,24},{24,16},{1,9},{9,1},{17,25},{25,17},{2,10},{10... | collective-permute-start | bytes 294920 | tf_op jit(solution)/shard_map/ppermute | solution.py:368
  3.7 2.6 %collective-permute-start.1 = (bf16[384,128]{1,0:T(8,128)(2,1)}, bf16[384,128]{1,0:T(8,128)(2,1)S(1)}, u32[]{:S(2)}, u32[]{:S(2)}) collective-permute-start(bf16[384,128]{1,0:T(8,128)(2,1)} %feat_hbm.1), channel_id=1, source_target_pairs={{0,16},{8,24},{16,0},{24,8},{1,17},{9,25},{17,1},{25,9},{2,18},{10... | collective-permute-start | bytes 294920 | tf_op jit(solution)/shard_map/ppermute | solution.py:368
  6.3 1.7 %collective-permute-start.9 = (bf16[384,128]{1,0:T(8,128)(2,1)}, bf16[384,128]{1,0:T(8,128)(2,1)S(1)}, u32[]{:S(2)}, u32[]{:S(2)}) collective-permute-start(bf16[384,128]{1,0:T(8,128)(2,1)} %cot_hbm.1), channel_id=1, source_target_pairs={{0,2},{1,3},{2,0},{3,1},{4,6},{5,7},{6,4},{7,5},{8,10},{9,11},{10,... | collective-permute-start | bytes 294920 | tf_op jit(solution)/shard_map/ppermute | solution.py:371
  8.1 1.5 %collective-permute-start.10 = (bf16[384,128]{1,0:T(8,128)(2,1)}, bf16[384,128]{1,0:T(8,128)(2,1)S(1)}, u32[]{:S(2)}, u32[]{:S(2)}) collective-permute-start(bf16[384,128]{1,0:T(8,128)(2,1)} %cot_hbm.1), channel_id=1, source_target_pairs={{0,4},{1,5},{2,6},{3,7},{4,0},{5,1},{6,2},{7,3},{8,12},{9,13},{10,... | collective-permute-start | bytes 294920 | tf_op jit(solution)/shard_map/ppermute | solution.py:371
  10.2 2.0 %shard_map.103 = (bf16[3072,1536]{1,0:T(8,128)(2,1)S(1)}, s32[8,512]{1,0:T(8,128)S(1)}, s32[8,512]{1,0:T(8,128)S(1)}, s32[8,384]{1,0:T(8,128)S(1)}, bf16[384,128...) custom-call(s32[1,256]{1,0:T(1,128)} %dest_hbm.1, s32[1,256]{1,0:T(1,128)} %src_hbm.1, s32[1,1]{1,0:T(1,128)S(6)} %copy.11.count_ref, ...), custom_call_target="tpu_custom_call" | custom-call | bytes 8388608 | tf_op jit(solution)/shard_map/pallas_call | solution.py:35
  15.7 1.4 %shard_map.105 = bf16[1536,128]{1,0:T(8,128)(2,1)S(1)} custom-call(bf16[3072,1536]{1,0:T(8,128)(2,1)S(1)} %get-tuple-element.35.dense_ref, bf16[384,128]{1,0:T(8,128)(2,1)S(1)} %get-tuple-element.38.refs_0_, bf16[384,128]{1,0:T(8,128)(2,1)S(1)} %collective-permute-done.refs_1_, bf16[384,128]{1,0:T(8,128)(2,1)S(1)} %collective-permute-done.1.refs_2_, ...), custom_call_target="tpu_custom_call" | custom-call | flops 603979776 | tf_op jit(solution)/shard_map/pallas_call | solution.py:35
  19.7 1.4 %shard_map.104.own_ref = bf16[1536,128]{1,0:T(8,128)(2,1)S(1)} custom-call(bf16[3072,1536]{1,0:T(8,128)(2,1)S(1)} %get-tuple-element.35.dense_ref, bf16[384,128]{1,0:T(8,128)(2,1)S(1)} %get-tuple-element.38.refs_0_, bf16[384,128]{1,0:T(8,128)(2,1)S(1)} %collective-permute-done.refs_1_, bf16[384,128]{1,0:T(8,128)(2,1)S(1)} %collective-permute-done.1.refs_2_, ...), custom_call_target="tpu_custom_call" | custom-call | flops 603979776 | tf_op jit(solution)/shard_map/pallas_call | solution.py:35
  21.8 1.6 %collective-permute-done.8 = s32[8,512]{1,0:T(8,128)S(1)} collective-permute-done((s32[8,512]{1,0:T(8,128)S(1)}, s32[8,512]{1,0:T(8,128)S(1)}, u32[]{:S(2)}, u32[]{:S(2)}) %collective-permute-start.8) | collective-permute-done | bytes 16416 | tf_op jit(solution)/shard_map/ppermute | solution.py:368
  23.4 1.5 %collective-permute-start.4 = (bf16[384,128]{1,0:T(8,128)(2,1)S(1)}, bf16[384,128]{1,0:T(8,128)(2,1)S(1)}, u32[]{:S(2)}, u32[]{:S(2)}) collective-permute-start(bf16[384,128]{1,0:T(8,128)(2,1)S(1)} %get-tuple-element.40), channel_id=1, source_target_pairs={{0,2},{1,3},{2,0},{3,1},{4,6},{5,7},{6,4},{7,5},{8,10},{9,11},{10,... | collective-permute-start | bytes 294920 | tf_op jit(solution)/shard_map/ppermute | solution.py:371
  24.9 1.5 %collective-permute-start.5 = (bf16[384,128]{1,0:T(8,128)(2,1)S(1)}, bf16[384,128]{1,0:T(8,128)(2,1)S(1)}, u32[]{:S(2)}, u32[]{:S(2)}) collective-permute-start(bf16[384,128]{1,0:T(8,128)(2,1)S(1)} %get-tuple-element.41), channel_id=1, source_target_pairs={{0,4},{1,5},{2,6},{3,7},{4,0},{5,1},{6,2},{7,3},{8,12},{9,13},{10,... | collective-permute-start | bytes 294920 | tf_op jit(solution)/shard_map/ppermute | solution.py:371
  27.3 1.3 %collective-permute-start.16 = (bf16[128,128]{1,0:T(8,128)(2,1)S(1)}, bf16[128,128]{1,0:T(8,128)(2,1)S(1)}, u32[]{:S(2)}, u32[]{:S(2)}) collective-permute-start(bf16[128,128]{1,0:T(8,128)(2,1)S(1)} %get-tuple-element.46), channel_id=1, source_target_pairs={{0,8},{8,0},{16,24},{24,16},{1,9},{9,1},{17,25},{25,17},{2,10},{10... | collective-permute-start | bytes 98312 | tf_op jit(solution)/shard_map/ppermute | solution.py:368
  28.6 1.8 %collective-permute-start.17 = (bf16[128,128]{1,0:T(8,128)(2,1)S(1)}, bf16[128,128]{1,0:T(8,128)(2,1)S(1)}, u32[]{:S(2)}, u32[]{:S(2)}) collective-permute-start(bf16[128,128]{1,0:T(8,128)(2,1)S(1)} %get-tuple-element.47), channel_id=1, source_target_pairs={{0,16},{8,24},{16,0},{24,8},{1,17},{9,25},{17,1},{25,9},{2,18},{10... | collective-permute-start | bytes 98312 | tf_op jit(solution)/shard_map/ppermute | solution.py:368
  31.3 2.4 %collective-permute-start.18 = (bf16[128,128]{1,0:T(8,128)(2,1)S(1)}, bf16[128,128]{1,0:T(8,128)(2,1)S(1)}, u32[]{:S(2)}, u32[]{:S(2)}) collective-permute-start(bf16[128,128]{1,0:T(8,128)(2,1)S(1)} %get-tuple-element.48), channel_id=1, source_target_pairs={{0,24},{8,16},{16,8},{24,0},{1,25},{9,17},{17,9},{25,1},{2,26},{10... | collective-permute-start | bytes 98312 | tf_op jit(solution)/shard_map/ppermute | solution.py:368
  34.0 3.1 %collective-permute-done.18.refs_7_ = bf16[128,128]{1,0:T(8,128)(2,1)S(1)} collective-permute-done((bf16[128,128]{1,0:T(8,128)(2,1)S(1)}, bf16[128,128]{1,0:T(8,128)(2,1)S(1)}, u32[]{:S(2)}, u32[]{:S(2)}) %collective-permute-start.18) | collective-permute-done | bytes 32800 | tf_op jit(solution)/shard_map/ppermute | solution.py:368
  37.8 1.6 %collective-permute-start.19 = (bf16[384,128]{1,0:T(8,128)(2,1)S(1)}, bf16[384,128]{1,0:T(8,128)(2,1)S(1)}, u32[]{:S(2)}, u32[]{:S(2)}) collective-permute-start(bf16[384,128]{1,0:T(8,128)(2,1)S(1)} %get-tuple-element.49.refs_0_), channel_id=1, source_target_pairs={{0,2},{1,3},{2,0},{3,1},{4,6},{5,7},{6,4},{7,5},{8,10},{9,11},{10,... | collective-permute-start | bytes 294920 | tf_op jit(solution)/shard_map/ppermute | solution.py:371
  39.4 1.7 %collective-permute-start.20 = (bf16[384,128]{1,0:T(8,128)(2,1)S(1)}, bf16[384,128]{1,0:T(8,128)(2,1)S(1)}, u32[]{:S(2)}, u32[]{:S(2)}) collective-permute-start(bf16[384,128]{1,0:T(8,128)(2,1)S(1)} %get-tuple-element.49.refs_0_), channel_id=1, source_target_pairs={{0,4},{1,5},{2,6},{3,7},{4,0},{5,1},{6,2},{7,3},{8,12},{9,13},{10,... | collective-permute-start | bytes 294920 | tf_op jit(solution)/shard_map/ppermute | solution.py:371
  41.4 3.1 %collective-permute-start.30 = (bf16[272,128]{1,0:T(8,128)(2,1)S(1)}, bf16[272,128]{1,0:T(8,128)(2,1)S(1)}, u32[]{:S(2)}, u32[]{:S(2)}) collective-permute-start(bf16[272,128]{1,0:T(8,128)(2,1)S(1)} %get-tuple-element.56), channel_id=1, source_target_pairs={{0,16},{8,24},{16,0},{24,8},{1,17},{9,25},{17,1},{25,9},{2,18},{10... | collective-permute-start | bytes 208904 | tf_op jit(solution)/shard_map/ppermute | solution.py:368
  46.8 3.8 %collective-permute-done.31.refs_3_ = bf16[272,128]{1,0:T(8,128)(2,1)S(1)} collective-permute-done((bf16[272,128]{1,0:T(8,128)(2,1)S(1)}, bf16[272,128]{1,0:T(8,128)(2,1)S(1)}, u32[]{:S(2)}, u32[]{:S(2)}) %collective-permute-start.31) | collective-permute-done | bytes 69664 | tf_op jit(solution)/shard_map/ppermute | solution.py:368
  52.7 1.7 %collective-permute-start.33 = (bf16[288,128]{1,0:T(8,128)(2,1)S(1)}, bf16[288,128]{1,0:T(8,128)(2,1)S(1)}, u32[]{:S(2)}, u32[]{:S(2)}) collective-permute-start(bf16[288,128]{1,0:T(8,128)(2,1)S(1)} %get-tuple-element.61), channel_id=1, source_target_pairs={{0,2},{1,3},{2,0},{3,1},{4,6},{5,7},{6,4},{7,5},{8,10},{9,11},{10,... | collective-permute-start | bytes 221192 | tf_op jit(solution)/shard_map/ppermute | solution.py:371
  55.7 1.7 %collective-permute-start.27 = (bf16[384,128]{1,0:T(8,128)(2,1)S(1)}, bf16[384,128]{1,0:T(8,128)(2,1)S(1)}, u32[]{:S(2)}, u32[]{:S(2)}) collective-permute-start(bf16[384,128]{1,0:T(8,128)(2,1)S(1)} %get-tuple-element.52), channel_id=1, source_target_pairs={{0,16},{8,24},{16,0},{24,8},{1,17},{9,25},{17,1},{25,9},{2,18},{10... | collective-permute-start | bytes 294920 | tf_op jit(solution)/shard_map/ppermute | solution.py:368
  57.4 2.7 %collective-permute-start.28 = (bf16[384,128]{1,0:T(8,128)(2,1)S(1)}, bf16[384,128]{1,0:T(8,128)(2,1)S(1)}, u32[]{:S(2)}, u32[]{:S(2)}) collective-permute-start(bf16[384,128]{1,0:T(8,128)(2,1)S(1)} %get-tuple-element.53), channel_id=1, source_target_pairs={{0,24},{8,16},{16,8},{24,0},{1,25},{9,17},{17,9},{25,1},{2,26},{10... | collective-permute-start | bytes 294920 | tf_op jit(solution)/shard_map/ppermute | solution.py:368
  60.1 1.8 %collective-permute-start.34 = (bf16[288,128]{1,0:T(8,128)(2,1)S(1)}, bf16[288,128]{1,0:T(8,128)(2,1)S(1)}, u32[]{:S(2)}, u32[]{:S(2)}) collective-permute-start(bf16[288,128]{1,0:T(8,128)(2,1)S(1)} %get-tuple-element.62), channel_id=1, source_target_pairs={{0,4},{1,5},{2,6},{3,7},{4,0},{5,1},{6,2},{7,3},{8,12},{9,13},{10,... | collective-permute-start | bytes 221192 | tf_op jit(solution)/shard_map/ppermute | solution.py:371
  62.0 2.5 %collective-permute-done.34.refs_6_ = bf16[288,128]{1,0:T(8,128)(2,1)S(1)} collective-permute-done((bf16[288,128]{1,0:T(8,128)(2,1)S(1)}, bf16[288,128]{1,0:T(8,128)(2,1)S(1)}, u32[]{:S(2)}, u32[]{:S(2)}) %collective-permute-start.34) | collective-permute-done | bytes 73760 | tf_op jit(solution)/shard_map/ppermute | solution.py:371
  64.5 2.7 %collective-permute-done.35.refs_7_ = bf16[288,128]{1,0:T(8,128)(2,1)S(1)} collective-permute-done((bf16[288,128]{1,0:T(8,128)(2,1)S(1)}, bf16[288,128]{1,0:T(8,128)(2,1)S(1)}, u32[]{:S(2)}, u32[]{:S(2)}) %collective-permute-start.35) | collective-permute-done | bytes 73760 | tf_op jit(solution)/shard_map/ppermute | solution.py:371
  (66 shorter events, 16.5 us)
Async XLA Ops:
  0.6 11.6 %collective-permute-start = (bf16[384,128]{1,0:T(8,128)(2,1)}, bf16[384,128]{1,0:T(8,128)(2,1)S(1)}, u32[]{:S(2)}, u32[]{:S(2)}) collective-permute-start(bf16[384,128]{1,0:T(8,128)(2,1)} %feat_hbm.1), channel_id=1, source_target_pairs={{0,8},{8,0},{16,24},{24,16},{1,9},{9,1},{17,25},{25,17},{2,10},{10... | collective-permute-start | bytes 294920 | tf_op jit(solution)/shard_map/ppermute | solution.py:368
  3.7 10.6 %collective-permute-start.1 = (bf16[384,128]{1,0:T(8,128)(2,1)}, bf16[384,128]{1,0:T(8,128)(2,1)S(1)}, u32[]{:S(2)}, u32[]{:S(2)}) collective-permute-start(bf16[384,128]{1,0:T(8,128)(2,1)} %feat_hbm.1), channel_id=1, source_target_pairs={{0,16},{8,24},{16,0},{24,8},{1,17},{9,25},{17,1},{25,9},{2,18},{10... | collective-permute-start | bytes 294920 | tf_op jit(solution)/shard_map/ppermute | solution.py:368
  6.3 9.3 %collective-permute-start.2 = (bf16[384,128]{1,0:T(8,128)(2,1)}, bf16[384,128]{1,0:T(8,128)(2,1)S(1)}, u32[]{:S(2)}, u32[]{:S(2)}) collective-permute-start(bf16[384,128]{1,0:T(8,128)(2,1)} %feat_hbm.1), channel_id=1, source_target_pairs={{0,24},{8,16},{16,8},{24,0},{1,25},{9,17},{17,9},{25,1},{2,26},{10... | collective-permute-start | bytes 294920 | tf_op jit(solution)/shard_map/ppermute | solution.py:368
  6.3 11.8 %collective-permute-start.9 = (bf16[384,128]{1,0:T(8,128)(2,1)}, bf16[384,128]{1,0:T(8,128)(2,1)S(1)}, u32[]{:S(2)}, u32[]{:S(2)}) collective-permute-start(bf16[384,128]{1,0:T(8,128)(2,1)} %cot_hbm.1), channel_id=1, source_target_pairs={{0,2},{1,3},{2,0},{3,1},{4,6},{5,7},{6,4},{7,5},{8,10},{9,11},{10,... | collective-permute-start | bytes 294920 | tf_op jit(solution)/shard_map/ppermute | solution.py:371
  8.1 10.6 %collective-permute-start.10 = (bf16[384,128]{1,0:T(8,128)(2,1)}, bf16[384,128]{1,0:T(8,128)(2,1)S(1)}, u32[]{:S(2)}, u32[]{:S(2)}) collective-permute-start(bf16[384,128]{1,0:T(8,128)(2,1)} %cot_hbm.1), channel_id=1, source_target_pairs={{0,4},{1,5},{2,6},{3,7},{4,0},{5,1},{6,2},{7,3},{8,12},{9,13},{10,... | collective-permute-start | bytes 294920 | tf_op jit(solution)/shard_map/ppermute | solution.py:371
  12.3 8.8 %collective-permute-start.11 = (bf16[384,128]{1,0:T(8,128)(2,1)}, bf16[384,128]{1,0:T(8,128)(2,1)S(1)}, u32[]{:S(2)}, u32[]{:S(2)}) collective-permute-start(bf16[384,128]{1,0:T(8,128)(2,1)} %cot_hbm.1), channel_id=1, source_target_pairs={{0,6},{1,7},{2,4},{3,5},{4,2},{5,3},{6,0},{7,1},{8,14},{9,15},{10,... | collective-permute-start | bytes 294920 | tf_op jit(solution)/shard_map/ppermute | solution.py:371
  18.1 6.7 %collective-permute-start.12 = (bf16[384,128]{1,0:T(8,128)(2,1)S(1)}, bf16[384,128]{1,0:T(8,128)(2,1)S(1)}, u32[]{:S(2)}, u32[]{:S(2)}) collective-permute-start(bf16[384,128]{1,0:T(8,128)(2,1)S(1)} %get-tuple-element.44.refs_0_), channel_id=1, source_target_pairs={{0,1},{1,0},{2,3},{3,2},{4,5},{5,4},{6,7},{7,6},{8,9},{9,8},{10,11... | collective-permute-start | bytes 294920 | tf_op jit(solution)/shard_map/ppermute | solution.py:371
  18.1 8.2 %collective-permute-start.13 = (bf16[384,128]{1,0:T(8,128)(2,1)S(1)}, bf16[384,128]{1,0:T(8,128)(2,1)S(1)}, u32[]{:S(2)}, u32[]{:S(2)}) collective-permute-start(bf16[384,128]{1,0:T(8,128)(2,1)S(1)} %collective-permute-done.9.refs_1_), channel_id=1, source_target_pairs={{0,1},{1,0},{2,3},{3,2},{4,5},{5,4},{6,7},{7,6},{8,9},{9,8},{10,11... | collective-permute-start | bytes 294920 | tf_op jit(solution)/shard_map/ppermute | solution.py:371
  21.1 5.7 %collective-permute-start.14 = (bf16[384,128]{1,0:T(8,128)(2,1)S(1)}, bf16[384,128]{1,0:T(8,128)(2,1)S(1)}, u32[]{:S(2)}, u32[]{:S(2)}) collective-permute-start(bf16[384,128]{1,0:T(8,128)(2,1)S(1)} %collective-permute-done.10.refs_2_), channel_id=1, source_target_pairs={{0,1},{1,0},{2,3},{3,2},{4,5},{5,4},{6,7},{7,6},{8,9},{9,8},{10,11... | collective-permute-start | bytes 294920 | tf_op jit(solution)/shard_map/ppermute | solution.py:371
  21.3 5.6 %collective-permute-start.15 = (bf16[384,128]{1,0:T(8,128)(2,1)S(1)}, bf16[384,128]{1,0:T(8,128)(2,1)S(1)}, u32[]{:S(2)}, u32[]{:S(2)}) collective-permute-start(bf16[384,128]{1,0:T(8,128)(2,1)S(1)} %collective-permute-done.11.refs_3_), channel_id=1, source_target_pairs={{0,1},{1,0},{2,3},{3,2},{4,5},{5,4},{6,7},{7,6},{8,9},{9,8},{10,11... | collective-permute-start | bytes 294920 | tf_op jit(solution)/shard_map/ppermute | solution.py:371
  23.4 13.8 %collective-permute-start.4 = (bf16[384,128]{1,0:T(8,128)(2,1)S(1)}, bf16[384,128]{1,0:T(8,128)(2,1)S(1)}, u32[]{:S(2)}, u32[]{:S(2)}) collective-permute-start(bf16[384,128]{1,0:T(8,128)(2,1)S(1)} %get-tuple-element.40), channel_id=1, source_target_pairs={{0,2},{1,3},{2,0},{3,1},{4,6},{5,7},{6,4},{7,5},{8,10},{9,11},{10,... | collective-permute-start | bytes 294920 | tf_op jit(solution)/shard_map/ppermute | solution.py:371
  24.9 12.3 %collective-permute-start.5 = (bf16[384,128]{1,0:T(8,128)(2,1)S(1)}, bf16[384,128]{1,0:T(8,128)(2,1)S(1)}, u32[]{:S(2)}, u32[]{:S(2)}) collective-permute-start(bf16[384,128]{1,0:T(8,128)(2,1)S(1)} %get-tuple-element.41), channel_id=1, source_target_pairs={{0,4},{1,5},{2,6},{3,7},{4,0},{5,1},{6,2},{7,3},{8,12},{9,13},{10,... | collective-permute-start | bytes 294920 | tf_op jit(solution)/shard_map/ppermute | solution.py:371
  26.4 10.8 %collective-permute-start.6 = (bf16[384,128]{1,0:T(8,128)(2,1)S(1)}, bf16[384,128]{1,0:T(8,128)(2,1)S(1)}, u32[]{:S(2)}, u32[]{:S(2)}) collective-permute-start(bf16[384,128]{1,0:T(8,128)(2,1)S(1)} %get-tuple-element.42), channel_id=1, source_target_pairs={{0,6},{1,7},{2,4},{3,5},{4,2},{5,3},{6,0},{7,1},{8,14},{9,15},{10,... | collective-permute-start | bytes 294920 | tf_op jit(solution)/shard_map/ppermute | solution.py:371
  28.6 5.4 %collective-permute-start.17 = (bf16[128,128]{1,0:T(8,128)(2,1)S(1)}, bf16[128,128]{1,0:T(8,128)(2,1)S(1)}, u32[]{:S(2)}, u32[]{:S(2)}) collective-permute-start(bf16[128,128]{1,0:T(8,128)(2,1)S(1)} %get-tuple-element.47), channel_id=1, source_target_pairs={{0,16},{8,24},{16,0},{24,8},{1,17},{9,25},{17,1},{25,9},{2,18},{10... | collective-permute-start | bytes 98312 | tf_op jit(solution)/shard_map/ppermute | solution.py:368
  31.3 5.8 %collective-permute-start.18 = (bf16[128,128]{1,0:T(8,128)(2,1)S(1)}, bf16[128,128]{1,0:T(8,128)(2,1)S(1)}, u32[]{:S(2)}, u32[]{:S(2)}) collective-permute-start(bf16[128,128]{1,0:T(8,128)(2,1)S(1)} %get-tuple-element.48), channel_id=1, source_target_pairs={{0,24},{8,16},{16,8},{24,0},{1,25},{9,17},{17,9},{25,1},{2,26},{10... | collective-permute-start | bytes 98312 | tf_op jit(solution)/shard_map/ppermute | solution.py:368
  37.8 6.7 %collective-permute-start.29 = (bf16[272,128]{1,0:T(8,128)(2,1)S(1)}, bf16[272,128]{1,0:T(8,128)(2,1)S(1)}, u32[]{:S(2)}, u32[]{:S(2)}) collective-permute-start(bf16[272,128]{1,0:T(8,128)(2,1)S(1)} %get-tuple-element.55), channel_id=1, source_target_pairs={{0,8},{8,0},{16,24},{24,16},{1,9},{9,1},{17,25},{25,17},{2,10},{10... | collective-permute-start | bytes 208904 | tf_op jit(solution)/shard_map/ppermute | solution.py:368
  37.8 13.4 %collective-permute-start.19 = (bf16[384,128]{1,0:T(8,128)(2,1)S(1)}, bf16[384,128]{1,0:T(8,128)(2,1)S(1)}, u32[]{:S(2)}, u32[]{:S(2)}) collective-permute-start(bf16[384,128]{1,0:T(8,128)(2,1)S(1)} %get-tuple-element.49.refs_0_), channel_id=1, source_target_pairs={{0,2},{1,3},{2,0},{3,1},{4,6},{5,7},{6,4},{7,5},{8,10},{9,11},{10,... | collective-permute-start | bytes 294920 | tf_op jit(solution)/shard_map/ppermute | solution.py:371
  39.4 11.9 %collective-permute-start.20 = (bf16[384,128]{1,0:T(8,128)(2,1)S(1)}, bf16[384,128]{1,0:T(8,128)(2,1)S(1)}, u32[]{:S(2)}, u32[]{:S(2)}) collective-permute-start(bf16[384,128]{1,0:T(8,128)(2,1)S(1)} %get-tuple-element.49.refs_0_), channel_id=1, source_target_pairs={{0,4},{1,5},{2,6},{3,7},{4,0},{5,1},{6,2},{7,3},{8,12},{9,13},{10,... | collective-permute-start | bytes 294920 | tf_op jit(solution)/shard_map/ppermute | solution.py:371
  41.1 10.7 %collective-permute-start.21 = (bf16[384,128]{1,0:T(8,128)(2,1)S(1)}, bf16[384,128]{1,0:T(8,128)(2,1)S(1)}, u32[]{:S(2)}, u32[]{:S(2)}) collective-permute-start(bf16[384,128]{1,0:T(8,128)(2,1)S(1)} %get-tuple-element.49.refs_0_), channel_id=1, source_target_pairs={{0,6},{1,7},{2,4},{3,5},{4,2},{5,3},{6,0},{7,1},{8,14},{9,15},{10,... | collective-permute-start | bytes 294920 | tf_op jit(solution)/shard_map/ppermute | solution.py:371
  44.5 6.1 %collective-permute-start.31 = (bf16[272,128]{1,0:T(8,128)(2,1)S(1)}, bf16[272,128]{1,0:T(8,128)(2,1)S(1)}, u32[]{:S(2)}, u32[]{:S(2)}) collective-permute-start(bf16[272,128]{1,0:T(8,128)(2,1)S(1)} %get-tuple-element.57), channel_id=1, source_target_pairs={{0,24},{8,16},{16,8},{24,0},{1,25},{9,17},{17,9},{25,1},{2,26},{10... | collective-permute-start | bytes 208904 | tf_op jit(solution)/shard_map/ppermute | solution.py:368
  52.7 9.2 %collective-permute-start.33 = (bf16[288,128]{1,0:T(8,128)(2,1)S(1)}, bf16[288,128]{1,0:T(8,128)(2,1)S(1)}, u32[]{:S(2)}, u32[]{:S(2)}) collective-permute-start(bf16[288,128]{1,0:T(8,128)(2,1)S(1)} %get-tuple-element.61), channel_id=1, source_target_pairs={{0,2},{1,3},{2,0},{3,1},{4,6},{5,7},{6,4},{7,5},{8,10},{9,11},{10,... | collective-permute-start | bytes 221192 | tf_op jit(solution)/shard_map/ppermute | solution.py:371
  55.0 12.2 %collective-permute-start.26 = (bf16[384,128]{1,0:T(8,128)(2,1)S(1)}, bf16[384,128]{1,0:T(8,128)(2,1)S(1)}, u32[]{:S(2)}, u32[]{:S(2)}) collective-permute-start(bf16[384,128]{1,0:T(8,128)(2,1)S(1)} %get-tuple-element.51), channel_id=1, source_target_pairs={{0,8},{8,0},{16,24},{24,16},{1,9},{9,1},{17,25},{25,17},{2,10},{10... | collective-permute-start | bytes 294920 | tf_op jit(solution)/shard_map/ppermute | solution.py:368
  55.7 11.5 %collective-permute-start.27 = (bf16[384,128]{1,0:T(8,128)(2,1)S(1)}, bf16[384,128]{1,0:T(8,128)(2,1)S(1)}, u32[]{:S(2)}, u32[]{:S(2)}) collective-permute-start(bf16[384,128]{1,0:T(8,128)(2,1)S(1)} %get-tuple-element.52), channel_id=1, source_target_pairs={{0,16},{8,24},{16,0},{24,8},{1,17},{9,25},{17,1},{25,9},{2,18},{10... | collective-permute-start | bytes 294920 | tf_op jit(solution)/shard_map/ppermute | solution.py:368
  57.4 9.7 %collective-permute-start.28 = (bf16[384,128]{1,0:T(8,128)(2,1)S(1)}, bf16[384,128]{1,0:T(8,128)(2,1)S(1)}, u32[]{:S(2)}, u32[]{:S(2)}) collective-permute-start(bf16[384,128]{1,0:T(8,128)(2,1)S(1)} %get-tuple-element.53), channel_id=1, source_target_pairs={{0,24},{8,16},{16,8},{24,0},{1,25},{9,17},{17,9},{25,1},{2,26},{10... | collective-permute-start | bytes 294920 | tf_op jit(solution)/shard_map/ppermute | solution.py:368
  (13 other events, 67.7 us)
